TPU v7x, 512 devices: a whole 4x8x8 slice. The times are simulated.
512 devices in a mesh: cuts: 32 (over x_hi, y, core), slab: 16 (over z, x_lo).
Axes of the slice: x: 4 (x_hi: 2, x_lo: 2; x = x_hi * 2 + x_lo), y: 8, z: 8, core: 2. Of those that a mesh axis runs over, the one named last changes fastest.
Arguments:
- orbitals: bfloat16 [1024, 64, 4096], P('cuts', 'slab'), may hold values from -0.25 to 0.25
- occupation: int32 [32, 32], P('cuts'), may hold values from 0 to 8
- state_counts: int32 [32], P('cuts'), may hold values from 8 to 32
- ion_charge: float32 [64, 4096], P('slab'), may hold values from 0.2 to 1.2, as said below
Outputs:
- potential: float32 [64, 4096], P('slab')
- kinetic: float32 [64, 4096], P('slab', 'cuts')
Inputs may be any that keep to these rules, and one draw needn't show every extreme that they name: `ion_charge`: the ionic charge is positive.
All inputs are finite; a program needn't handle non-finite values.
Results may differ from a plain program's by a relative error of at most 0.0003.
Values may be sent and summed in bfloat16 or wider, within the bound.
A program may use at most 64 MiB of HBM per device.

v0:
```python
import jax
import jax.numpy as jnp
from jax import lax
from jax.sharding import PartitionSpec as P

NX = 64
LEVELS = 3
CYCLES = 2
COARSE_SWEEPS = 4
OCC_DEN = 8


OMEGA = 0.8
COUPLING = 4.0


def extended(array, sides, width):
    for axis, dim in sides:
        size, length = (lax.axis_size(axis), array.shape[dim])
        up = [(i, (i + 1) % size) for i in range(size - 1)]
        down = [(j, i) for i, j in up]
        last = lax.slice_in_dim(array, length - width, length, axis=dim)
        leading = lax.slice_in_dim(array, 0, width, axis=dim)
        before = lax.ppermute(last, axis, up)
        after = lax.ppermute(leading, axis, down)
        array = jnp.concatenate([before, array, after], axis=dim)
    return array


def sent_to_all(array, axis):
    length = lax.axis_size(axis)
    return lax.all_to_all(
        jnp.broadcast_to(array[None], (length, *array.shape)), axis, 0, 0, tiled=True
    )


def in_order(parts, dim):
    shape = list(parts.shape[1:])
    shape[dim] *= parts.shape[0]
    return jnp.moveaxis(parts, 0, dim).reshape(shape)


def gather_directly(array, axis, dim):
    parts = sent_to_all(array, axis)
    return in_order(parts, dim)


def in_blocks(array, dim, length):
    before, after = (array.shape[:dim], array.shape[dim + 1 :])
    return jnp.moveaxis(array.reshape(*before, length, -1, *after), dim, 0)


def sum_at_owner(array, axis, dim):
    parts = in_blocks(array, dim, lax.axis_size(axis))
    arrived = lax.all_to_all(parts, axis, split_axis=0, concat_axis=0, tiled=True)
    return arrived.sum(axis=0)


def in_one_piece(arrays, axis, dim, along):
    both = jnp.concatenate(arrays, axis=along)
    result, at, gathered = (sum_at_owner(both, axis, dim), 0, [])
    for a in arrays:
        gathered.append(lax.slice_in_dim(result, at, at + a.shape[along], axis=along))
        at += a.shape[along]
    return tuple(gathered)


def take_next(values, offset):
    padding = [(0, 0)] * (values.ndim - 1) + [(0, offset)]
    return jnp.pad(values[..., offset:], padding)


def take_prev(values, offset):
    padding = [(0, 0)] * (values.ndim - 1) + [(offset, 0)]
    return jnp.pad(values[..., :-offset], padding)


def x_neighbours(values, side_cells):
    column = jnp.arange(values.shape[-1]) % side_cells
    next_cell = jnp.where(column != side_cells - 1, take_next(values, 1), 0.0)
    prev_cell = jnp.where(column != 0, take_prev(values, 1), 0.0)
    return (next_cell, prev_cell)


def plane_sum(values, side_cells):
    next_cell, prev_cell = x_neighbours(values, side_cells)
    return next_cell + prev_cell + take_next(values, side_cells) + take_prev(values, side_cells)


def stencil(iterate, padded, side_cells, degree):
    return (
        6.0 * iterate - plane_sum(iterate, side_cells) - padded[2:] - padded[:-2]
    ) * 0.25**degree


def smooth(iterate, forcing, padded, side_cells, degree):
    return iterate + OMEGA * 4.0**degree / 6.0 * (
        forcing - stencil(iterate, padded, side_cells, degree)
    )


def restrict(residual, side_cells):
    planes = residual.shape[0]
    half_cells = side_cells // 2
    blocks = residual.reshape(planes // 2, 2, half_cells, 2, half_cells, 2)
    return jnp.mean(blocks, axis=(1, 3, 5)).reshape(planes // 2, half_cells * half_cells)


def prolong(coarse, half_cells):
    planes = coarse.shape[0]
    spread = jnp.broadcast_to(
        coarse.reshape(planes, 1, half_cells, 1, half_cells, 1),
        (planes, 2, half_cells, 2, half_cells, 2),
    )
    return spread.reshape(2 * planes, 4 * half_cells * half_cells)


def pad_planes(iterate):
    return jnp.pad(iterate, ((1, 1), (0, 0)))


def grid_rims(iterate):
    return extended(iterate, (("slab", 0),), 1)


def coarse_solve(forcing, side_cells):
    degree = LEVELS - 1
    whole_source = gather_directly(forcing, "slab", 0)
    iterate = jnp.zeros_like(whole_source)
    for sweep_index in range(COARSE_SWEEPS):
        iterate = smooth(iterate, whole_source, pad_planes(iterate), side_cells, degree)
    own_rows = forcing.shape[0]
    return lax.dynamic_slice_in_dim(iterate, lax.axis_index("slab") * own_rows, own_rows, 0)


def vcycle(degree, iterate, forcing, side_cells):
    if degree == LEVELS - 1:
        return coarse_solve(forcing, side_cells)
    iterate = smooth(iterate, forcing, grid_rims(iterate), side_cells, degree)
    residual = forcing - stencil(iterate, grid_rims(iterate), side_cells, degree)
    coarse_forcing = restrict(residual, side_cells)
    correction = vcycle(degree + 1, jnp.zeros_like(coarse_forcing), coarse_forcing, side_cells // 2)
    iterate = iterate + prolong(correction, side_cells // 2)
    return smooth(iterate, forcing, grid_rims(iterate), side_cells, degree)


def live_weights(occupation_row, live_count):
    ranks = jnp.arange(occupation_row.shape[0])
    return jnp.where(ranks < live_count, occupation_row.astype(jnp.float32) / OCC_DEN, 0.0)


def orbital_terms(padded, weights, side_cells):
    states, planes, cells = padded.shape
    block_rows = 8
    blocks = padded.reshape(states // block_rows, block_rows, planes, cells)
    block_weights = weights.reshape(states // block_rows, block_rows)

    def accumulate(totals, items):
        piece, piece_weights = items
        values = piece.astype(jnp.float32)
        interior = values[:, 1:-1]
        next_cell, prev_cell = x_neighbours(interior, side_cells)
        slope_x = (next_cell - prev_cell) * 0.5
        slope_y = (take_next(interior, side_cells) - take_prev(interior, side_cells)) * 0.5
        slope_z = (values[:, 2:] - values[:, :-2]) * 0.5
        density = jnp.einsum(
            "s,szf->zf", piece_weights, interior * interior, precision=lax.Precision.HIGHEST
        )
        squares = slope_x * slope_x + slope_y * slope_y + slope_z * slope_z
        kinetic = 0.5 * jnp.einsum(
            "s,szf->zf", piece_weights, squares, precision=lax.Precision.HIGHEST
        )
        return ((totals[0] + density, totals[1] + kinetic), None)

    zero_field = jnp.zeros((planes - 2, cells), jnp.float32)
    (density, kinetic), unused = lax.scan(
        accumulate, (zero_field, zero_field), (blocks, block_weights)
    )
    return (density, kinetic)


def shards(orbitals, occupation, state_counts, ion_charge):
    padded = extended(orbitals, (("slab", 1),), 1)
    weights = live_weights(occupation[0], state_counts[0])
    density, kinetic = orbital_terms(padded, weights, NX)
    density_part, kinetic = in_one_piece((density, kinetic), "cuts", 1, 0)
    density = gather_directly(density_part, "cuts", 1)
    forcing = COUPLING * (density - ion_charge)
    potential = jnp.zeros_like(forcing)
    for repeat in range(CYCLES):
        potential = vcycle(0, potential, forcing, NX)
    return (potential, kinetic)


def solution(mesh):
    return jax.shard_map(
        shards,
        mesh=mesh,
        in_specs=(P("cuts", "slab", None), P("cuts", None), P("cuts"), P("slab", None)),
        out_specs=(P("slab", None), P("slab", "cuts")),
        check_vma=False,
    )
```

profile of v0, /device:TPU:64, one launch (start us, length us, event | category | flops | bytes accessed | tf_op | source)
XLA Modules:
  0.0 244.0 jit_solution(11085467126310689957)
XLA Ops:
  0.6 2.8 %fusion.117 = (bf16[32,1,4096]{2,1,0:T(2,128)(2,1)S(1)}, bf16[32,1,4096]{2,1,0:T(2,128)(2,1)S(1)}) fusion(bf16[32,4,4096]{2,1,0:T(4,128)(2,1)} %param.6), kind=kLoop, calls=%fused_computation.197 | loop fusion | bytes 1048576 | tf_op jit(solution)/shard_map/slice | solution.py:22
  3.8 3.4 %collective-permute-start = (bf16[32,1,4096]{2,0,1:T(8,128)(2,1)S(1)}, bf16[32,1,4096]{2,0,1:T(8,128)(2,1)S(1)}, u32[]{:S(2)}, u32[]{:S(2)}) collective-permute-start(bf16[32,1,4096]{2,0,1:T(8,128)(2,1)S(1)} %copy.16), channel_id=1, source_target_pairs={{0,1},{1,2},{2,3},{3,4},{4,5},{5,6},{6,7},{7,8},{8,9},{9,10},{10,1... | collective-permute-start | bytes 786440 | tf_op jit(solution)/shard_map/ppermute | solution.py:24
  7.5 3.3 %collective-permute-start.1 = (bf16[32,1,4096]{2,0,1:T(8,128)(2,1)S(1)}, bf16[32,1,4096]{2,0,1:T(8,128)(2,1)S(1)}, u32[]{:S(2)}, u32[]{:S(2)}) collective-permute-start(bf16[32,1,4096]{2,0,1:T(8,128)(2,1)S(1)} %copy.17), channel_id=1, source_target_pairs={{1,0},{2,1},{3,2},{4,3},{5,4},{6,5},{7,6},{8,7},{9,8},{10,9},{11,1... | collective-permute-start | bytes 786440 | tf_op jit(solution)/shard_map/ppermute | solution.py:25
  12.3 6.1 %collective-permute-done = bf16[32,1,4096]{2,0,1:T(8,128)(2,1)S(1)} collective-permute-done((bf16[32,1,4096]{2,0,1:T(8,128)(2,1)S(1)}, bf16[32,1,4096]{2,0,1:T(8,128)(2,1)S(1)}, u32[]{:S(2)}, u32[]{:S(2)}) %collective-permute-start) | collective-permute-done | bytes 262176 | tf_op jit(solution)/shard_map/ppermute | solution.py:24
  22.5 14.3 %while.15 = (s32[]{:T(128)}, f32[4,4096]{1,0:T(4,128)S(1)}, f32[4,4096]{1,0:T(4,128)S(1)}, f32[4,8]{1,0:T(4,128)S(1)}, bf16[4,8,6,4096]{3,2,1,0:T(8,128)(2,1)S(1)}, /*index=5*/s32[]{:T(128)}, s32[]{:T(128)}) while((s32[]{:T(128)}, f32[4,4096]{1,0:T(4,128)S(1)}, f32[4,4096]{1,0:T(4,128)S(1)}, f32[4,8]{1,0:T(4,128)S(1)}, ...), condition=%wide.region_1.2_spmd.clone, body=%wide.region_0.1_spmd.clone.sunk | while | flops 5316611 | bytes 11632995 | solution.py:176
  37.6 10.0 %all-to-all-start = ((f32[32,8,128]{2,1,0:T(8,128)}), f32[32,8,128]{2,1,0:T(8,128)S(1)}, u32[]{:S(2)}, u32[]{:S(2)}) async-start(f32[32,8,128]{2,1,0:T(8,128)} %maximum_bitcast_fusion), calls=%async_computation | async-start | bytes 262144 | tf_op jit(solution)/shard_map/all_to_all | solution.py:55
  49.5 3.9 %collective-permute-start.3 = (f32[1,4096]{1,0:T(1,128)S(1)}, f32[1,4096]{1,0:T(1,128)S(1)}, u32[]{:S(2)}, u32[]{:S(2)}) collective-permute-start(f32[1,4096]{1,0:T(1,128)S(1)} %broadcast.348), channel_id=1, source_target_pairs={{0,1},{1,2},{2,3},{3,4},{4,5},{5,6},{6,7},{7,8},{8,9},{9,10},{10,1... | collective-permute-start | bytes 49160 | tf_op jit(solution)/shard_map/ppermute | solution.py:24
  56.2 3.0 %collective-permute-start.7 = (f32[1,1024]{1,0:T(1,128)S(1)}, f32[1,1024]{1,0:T(1,128)S(1)}, u32[]{:S(2)}, u32[]{:S(2)}) collective-permute-start(f32[1,1024]{1,0:T(1,128)S(1)} %broadcast.354), channel_id=1, source_target_pairs={{0,1},{1,2},{2,3},{3,4},{4,5},{5,6},{6,7},{7,8},{8,9},{9,10},{10,1... | collective-permute-start | bytes 12296 | tf_op jit(solution)/shard_map/ppermute | solution.py:24
  60.7 9.6 %all-to-all-start.1 = ((f32[32,4,128]{2,1,0:T(4,128)}), f32[32,4,128]{2,1,0:T(4,128)S(1)}, u32[]{:S(2)}, u32[]{:S(2)}) async-start(f32[32,4,128]{2,1,0:T(4,128)} %broadcast_in_dim.236), calls=%async_computation.1 | async-start | bytes 131072 | tf_op jit(solution)/shard_map/all_to_all | solution.py:32
  70.4 10.5 %all-to-all-done.1 = f32[32,4,128]{2,1,0:T(4,128)S(1)} async-done(((f32[32,4,128]{2,1,0:T(4,128)}), f32[32,4,128]{2,1,0:T(4,128)S(1)}, u32[]{:S(2)}, u32[]{:S(2)}) %all-to-all-start.1) | async-done | bytes 65568 | tf_op jit(solution)/shard_map/all_to_all | solution.py:32
  81.2 3.1 %collective-permute-start.4 = (f32[1,4096]{1,0:T(1,128)S(1)}, f32[1,4096]{1,0:T(1,128)S(1)}, u32[]{:S(2)}, u32[]{:S(2)}) collective-permute-start(f32[1,4096]{1,0:T(1,128)S(1)} %get-tuple-element.143), channel_id=1, source_target_pairs={{1,0},{2,1},{3,2},{4,3},{5,4},{6,5},{7,6},{8,7},{9,8},{10,9},{11,1... | collective-permute-start | bytes 49160 | tf_op jit(solution)/shard_map/ppermute | solution.py:25
  84.4 3.0 %collective-permute-start.5 = (f32[1,4096]{1,0:T(1,128)S(1)}, f32[1,4096]{1,0:T(1,128)S(1)}, u32[]{:S(2)}, u32[]{:S(2)}) collective-permute-start(f32[1,4096]{1,0:T(1,128)S(1)} %get-tuple-element.144), channel_id=1, source_target_pairs={{0,1},{1,2},{2,3},{3,4},{4,5},{5,6},{6,7},{7,8},{8,9},{9,10},{10,1... | collective-permute-start | bytes 49160 | tf_op jit(solution)/shard_map/ppermute | solution.py:24
  87.5 3.4 %collective-permute-done.5 = f32[1,4096]{1,0:T(1,128)S(1)} collective-permute-done((f32[1,4096]{1,0:T(1,128)S(1)}, f32[1,4096]{1,0:T(1,128)S(1)}, u32[]{:S(2)}, u32[]{:S(2)}) %collective-permute-start.5) | collective-permute-done | bytes 16416 | tf_op jit(solution)/shard_map/ppermute | solution.py:24
  91.1 6.3 %reshape.97 = f32[2,2,32,2,32,2]{5,4,3,2,1,0:T(8,128)} reshape(f32[4,4096]{1,0:T(4,128)S(1)} %fusion.37) | data formatting | bytes 131072 | tf_op jit(solution)/shard_map/reshape | solution.py:105
  102.2 3.9 %collective-permute-start.9 = (f32[1,1024]{1,0:T(1,128)S(1)}, f32[1,1024]{1,0:T(1,128)S(1)}, u32[]{:S(2)}, u32[]{:S(2)}) collective-permute-start(f32[1,1024]{1,0:T(1,128)S(1)} %get-tuple-element.198), channel_id=1, source_target_pairs={{0,1},{1,2},{2,3},{3,4},{4,5},{5,6},{6,7},{7,8},{8,9},{9,10},{10,1... | collective-permute-start | bytes 12296 | tf_op jit(solution)/shard_map/ppermute | solution.py:24
  109.8 16.4 %all-to-all-start.2 = ((f32[16,1,256]{2,1,0:T(1,128)}), f32[16,1,256]{2,1,0:T(1,128)S(1)}, u32[]{:S(2)}, u32[]{:S(2)}) async-start(f32[16,1,256]{2,1,0:T(1,128)} %broadcast_in_dim.241), calls=%async_computation.2 | async-start | bytes 32768 | tf_op jit(solution)/shard_map/all_to_all | solution.py:32
  126.2 7.2 %all-to-all-done.2 = f32[16,1,256]{2,1,0:T(1,128)S(1)} async-done(((f32[16,1,256]{2,1,0:T(1,128)}), f32[16,1,256]{2,1,0:T(1,128)S(1)}, u32[]{:S(2)}, u32[]{:S(2)}) %all-to-all-start.2) | async-done | bytes 16416 | tf_op jit(solution)/shard_map/all_to_all | solution.py:32
  134.8 3.3 %collective-permute-start.10 = (f32[1,1024]{1,0:T(1,128)S(1)}, f32[1,1024]{1,0:T(1,128)S(1)}, u32[]{:S(2)}, u32[]{:S(2)}) collective-permute-start(f32[1,1024]{1,0:T(1,128)S(1)} %get-tuple-element.191), channel_id=1, source_target_pairs={{1,0},{2,1},{3,2},{4,3},{5,4},{6,5},{7,6},{8,7},{9,8},{10,9},{11,1... | collective-permute-start | bytes 12296 | tf_op jit(solution)/shard_map/ppermute | solution.py:25
  140.7 3.8 %collective-permute-done.11 = f32[1,1024]{1,0:T(1,128)S(1)} collective-permute-done((f32[1,1024]{1,0:T(1,128)S(1)}, f32[1,1024]{1,0:T(1,128)S(1)}, u32[]{:S(2)}, u32[]{:S(2)}) %collective-permute-start.11) | collective-permute-done | bytes 4128 | tf_op jit(solution)/shard_map/ppermute | solution.py:24
  147.3 5.4 %reshape.99 = f32[4,4096]{1,0:T(4,128)S(1)} reshape(f32[2,2,32,2,32,2]{5,4,3,2,1,0:T(8,128)} %broadcast_in_dim.249) | data formatting | bytes 131072 | tf_op jit(solution)/shard_map/reshape | solution.py:115
  155.4 3.4 %collective-permute-start.13 = (f32[1,4096]{1,0:T(1,128)S(1)}, f32[1,4096]{1,0:T(1,128)S(1)}, u32[]{:S(2)}, u32[]{:S(2)}) collective-permute-start(f32[1,4096]{1,0:T(1,128)S(1)} %get-tuple-element.138), channel_id=1, source_target_pairs={{0,1},{1,2},{2,3},{3,4},{4,5},{5,6},{6,7},{7,8},{8,9},{9,10},{10,1... | collective-permute-start | bytes 49160 | tf_op jit(solution)/shard_map/ppermute | solution.py:24
  158.9 3.0 %collective-permute-done.13 = f32[1,4096]{1,0:T(1,128)S(1)} collective-permute-done((f32[1,4096]{1,0:T(1,128)S(1)}, f32[1,4096]{1,0:T(1,128)S(1)}, u32[]{:S(2)}, u32[]{:S(2)}) %collective-permute-start.13) | collective-permute-done | bytes 16416 | tf_op jit(solution)/shard_map/ppermute | solution.py:24
  164.1 3.9 %collective-permute-start.15 = (f32[1,4096]{1,0:T(1,128)S(1)}, f32[1,4096]{1,0:T(1,128)S(1)}, u32[]{:S(2)}, u32[]{:S(2)}) collective-permute-start(f32[1,4096]{1,0:T(1,128)S(1)} %get-tuple-element.132), channel_id=1, source_target_pairs={{0,1},{1,2},{2,3},{3,4},{4,5},{5,6},{6,7},{7,8},{8,9},{9,10},{10,1... | collective-permute-start | bytes 49160 | tf_op jit(solution)/shard_map/ppermute | solution.py:24
  172.9 4.1 %collective-permute-start.17 = (f32[1,4096]{1,0:T(1,128)S(1)}, f32[1,4096]{1,0:T(1,128)S(1)}, u32[]{:S(2)}, u32[]{:S(2)}) collective-permute-start(f32[1,4096]{1,0:T(1,128)S(1)} %get-tuple-element.126), channel_id=1, source_target_pairs={{0,1},{1,2},{2,3},{3,4},{4,5},{5,6},{6,7},{7,8},{8,9},{9,10},{10,1... | collective-permute-start | bytes 49160 | tf_op jit(solution)/shard_map/ppermute | solution.py:24
  179.6 6.3 %reshape.100 = f32[2,2,32,2,32,2]{5,4,3,2,1,0:T(8,128)} reshape(f32[4,4096]{1,0:T(4,128)S(1)} %fusion.24) | data formatting | bytes 131072 | tf_op jit(solution)/shard_map/reshape | solution.py:105
  190.6 3.9 %collective-permute-start.19 = (f32[1,1024]{1,0:T(1,128)S(1)}, f32[1,1024]{1,0:T(1,128)S(1)}, u32[]{:S(2)}, u32[]{:S(2)}) collective-permute-start(f32[1,1024]{1,0:T(1,128)S(1)} %get-tuple-element.186), channel_id=1, source_target_pairs={{0,1},{1,2},{2,3},{3,4},{4,5},{5,6},{6,7},{7,8},{8,9},{9,10},{10,1... | collective-permute-start | bytes 12296 | tf_op jit(solution)/shard_map/ppermute | solution.py:24
  197.6 17.2 %all_to_all.20 = f32[16,1,256]{2,1,0:T(1,128)S(1)} all-to-all(f32[16,1,256]{2,1,0:T(1,128)S(1)} %broadcast_in_dim.250), channel_id=1, replica_groups=mesh['cuts'=32,'slab'=16] {'slab'}, dimensions={0} | all-to-all | bytes 32768 | tf_op jit(solution)/shard_map/all_to_all | solution.py:32
  216.0 3.3 %collective-permute-start.20 = (f32[1,1024]{1,0:T(1,128)S(1)}, f32[1,1024]{1,0:T(1,128)S(1)}, u32[]{:S(2)}, u32[]{:S(2)}) collective-permute-start(f32[1,1024]{1,0:T(1,128)S(1)} %get-tuple-element.179), channel_id=1, source_target_pairs={{1,0},{2,1},{3,2},{4,3},{5,4},{6,5},{7,6},{8,7},{9,8},{10,9},{11,1... | collective-permute-start | bytes 12296 | tf_op jit(solution)/shard_map/ppermute | solution.py:25
  222.0 3.8 %collective-permute-done.21 = f32[1,1024]{1,0:T(1,128)S(1)} collective-permute-done((f32[1,1024]{1,0:T(1,128)S(1)}, f32[1,1024]{1,0:T(1,128)S(1)}, u32[]{:S(2)}, u32[]{:S(2)}) %collective-permute-start.21) | collective-permute-done | bytes 4128 | tf_op jit(solution)/shard_map/ppermute | solution.py:24
  228.6 5.4 %reshape.102 = f32[4,4096]{1,0:T(4,128)S(1)} reshape(f32[2,2,32,2,32,2]{5,4,3,2,1,0:T(8,128)} %broadcast_in_dim.256) | data formatting | bytes 131072 | tf_op jit(solution)/shard_map/reshape | solution.py:115
  236.6 3.4 %collective-permute-start.23 = (f32[1,4096]{1,0:T(1,128)S(1)}, f32[1,4096]{1,0:T(1,128)S(1)}, u32[]{:S(2)}, u32[]{:S(2)}) collective-permute-start(f32[1,4096]{1,0:T(1,128)S(1)} %get-tuple-element.120), channel_id=1, source_target_pairs={{0,1},{1,2},{2,3},{3,4},{4,5},{5,6},{6,7},{7,8},{8,9},{9,10},{10,1... | collective-permute-start | bytes 49160 | tf_op jit(solution)/shard_map/ppermute | solution.py:24
  240.1 3.0 %collective-permute-done.23 = f32[1,4096]{1,0:T(1,128)S(1)} collective-permute-done((f32[1,4096]{1,0:T(1,128)S(1)}, f32[1,4096]{1,0:T(1,128)S(1)}, u32[]{:S(2)}, u32[]{:S(2)}) %collective-permute-start.23) | collective-permute-done | bytes 16416 | tf_op jit(solution)/shard_map/ppermute | solution.py:24
  (188 shorter events, 71.9 us)
Async XLA Ops:
  0.6 20.2 %copy-start = (bf16[32,4,4096]{2,1,0:T(4,128)(2,1)S(1)}, bf16[32,4,4096]{2,1,0:T(4,128)(2,1)}, u32[]{:S(2)}) copy-start(bf16[32,4,4096]{2,1,0:T(4,128)(2,1)} %param.6) | copy-start | bytes 3145732
  3.8 14.6 %collective-permute-start = (bf16[32,1,4096]{2,0,1:T(8,128)(2,1)S(1)}, bf16[32,1,4096]{2,0,1:T(8,128)(2,1)S(1)}, u32[]{:S(2)}, u32[]{:S(2)}) collective-permute-start(bf16[32,1,4096]{2,0,1:T(8,128)(2,1)S(1)} %copy.16), channel_id=1, source_target_pairs={{0,1},{1,2},{2,3},{3,4},{4,5},{5,6},{6,7},{7,8},{8,9},{9,10},{10,1... | collective-permute-start | bytes 786440 | tf_op jit(solution)/shard_map/ppermute | solution.py:24
  7.5 12.7 %collective-permute-start.1 = (bf16[32,1,4096]{2,0,1:T(8,128)(2,1)S(1)}, bf16[32,1,4096]{2,0,1:T(8,128)(2,1)S(1)}, u32[]{:S(2)}, u32[]{:S(2)}) collective-permute-start(bf16[32,1,4096]{2,0,1:T(8,128)(2,1)S(1)} %copy.17), channel_id=1, source_target_pairs={{1,0},{2,1},{3,2},{4,3},{5,4},{6,5},{7,6},{8,7},{9,8},{10,9},{11,1... | collective-permute-start | bytes 786440 | tf_op jit(solution)/shard_map/ppermute | solution.py:25
  22.5 58.4 %copy-start.1 = (f32[4,4096]{1,0:T(4,128)S(1)}, f32[4,4096]{1,0:T(4,128)}, u32[]{:S(2)}) copy-start(f32[4,4096]{1,0:T(4,128)} %param.9) | copy-start | bytes 196612
  37.6 21.9 %all-to-all-start = ((f32[32,8,128]{2,1,0:T(8,128)}), f32[32,8,128]{2,1,0:T(8,128)S(1)}, u32[]{:S(2)}, u32[]{:S(2)}) async-start(f32[32,8,128]{2,1,0:T(8,128)} %maximum_bitcast_fusion), calls=%async_computation | async-start | bytes 262144 | tf_op jit(solution)/shard_map/all_to_all | solution.py:55
  47.5 22.9 %collective-permute-start.2 = (f32[1,4096]{1,0:T(1,128)S(1)}, f32[1,4096]{1,0:T(1,128)S(1)}, u32[]{:S(2)}, u32[]{:S(2)}) collective-permute-start(f32[1,4096]{1,0:T(1,128)S(1)} %broadcast.348), channel_id=1, source_target_pairs={{1,0},{2,1},{3,2},{4,3},{5,4},{6,5},{7,6},{8,7},{9,8},{10,9},{11,1... | collective-permute-start | bytes 49160 | tf_op jit(solution)/shard_map/ppermute | solution.py:25
  49.5 20.9 %collective-permute-start.3 = (f32[1,4096]{1,0:T(1,128)S(1)}, f32[1,4096]{1,0:T(1,128)S(1)}, u32[]{:S(2)}, u32[]{:S(2)}) collective-permute-start(f32[1,4096]{1,0:T(1,128)S(1)} %broadcast.348), channel_id=1, source_target_pairs={{0,1},{1,2},{2,3},{3,4},{4,5},{5,6},{6,7},{7,8},{8,9},{9,10},{10,1... | collective-permute-start | bytes 49160 | tf_op jit(solution)/shard_map/ppermute | solution.py:24
  53.4 46.7 %collective-permute-start.6 = (f32[1,1024]{1,0:T(1,128)S(1)}, f32[1,1024]{1,0:T(1,128)S(1)}, u32[]{:S(2)}, u32[]{:S(2)}) collective-permute-start(f32[1,1024]{1,0:T(1,128)S(1)} %broadcast.354), channel_id=1, source_target_pairs={{1,0},{2,1},{3,2},{4,3},{5,4},{6,5},{7,6},{8,7},{9,8},{10,9},{11,1... | collective-permute-start | bytes 12296 | tf_op jit(solution)/shard_map/ppermute | solution.py:25
  56.2 43.8 %collective-permute-start.7 = (f32[1,1024]{1,0:T(1,128)S(1)}, f32[1,1024]{1,0:T(1,128)S(1)}, u32[]{:S(2)}, u32[]{:S(2)}) collective-permute-start(f32[1,1024]{1,0:T(1,128)S(1)} %broadcast.354), channel_id=1, source_target_pairs={{0,1},{1,2},{2,3},{3,4},{4,5},{5,6},{6,7},{7,8},{8,9},{9,10},{10,1... | collective-permute-start | bytes 12296 | tf_op jit(solution)/shard_map/ppermute | solution.py:24
  60.7 20.2 %all-to-all-start.1 = ((f32[32,4,128]{2,1,0:T(4,128)}), f32[32,4,128]{2,1,0:T(4,128)S(1)}, u32[]{:S(2)}, u32[]{:S(2)}) async-start(f32[32,4,128]{2,1,0:T(4,128)} %broadcast_in_dim.236), calls=%async_computation.1 | async-start | bytes 131072 | tf_op jit(solution)/shard_map/all_to_all | solution.py:32
  81.2 6.2 %collective-permute-start.4 = (f32[1,4096]{1,0:T(1,128)S(1)}, f32[1,4096]{1,0:T(1,128)S(1)}, u32[]{:S(2)}, u32[]{:S(2)}) collective-permute-start(f32[1,4096]{1,0:T(1,128)S(1)} %get-tuple-element.143), channel_id=1, source_target_pairs={{1,0},{2,1},{3,2},{4,3},{5,4},{6,5},{7,6},{8,7},{9,8},{10,9},{11,1... | collective-permute-start | bytes 49160 | tf_op jit(solution)/shard_map/ppermute | solution.py:25
  84.4 6.5 %collective-permute-start.5 = (f32[1,4096]{1,0:T(1,128)S(1)}, f32[1,4096]{1,0:T(1,128)S(1)}, u32[]{:S(2)}, u32[]{:S(2)}) collective-permute-start(f32[1,4096]{1,0:T(1,128)S(1)} %get-tuple-element.144), channel_id=1, source_target_pairs={{0,1},{1,2},{2,3},{3,4},{4,5},{5,6},{6,7},{7,8},{8,9},{9,10},{10,1... | collective-permute-start | bytes 49160 | tf_op jit(solution)/shard_map/ppermute | solution.py:24
  100.3 5.9 %collective-permute-start.8 = (f32[1,1024]{1,0:T(1,128)S(1)}, f32[1,1024]{1,0:T(1,128)S(1)}, u32[]{:S(2)}, u32[]{:S(2)}) collective-permute-start(f32[1,1024]{1,0:T(1,128)S(1)} %get-tuple-element.197), channel_id=1, source_target_pairs={{1,0},{2,1},{3,2},{4,3},{5,4},{6,5},{7,6},{8,7},{9,8},{10,9},{11,1... | collective-permute-start | bytes 12296 | tf_op jit(solution)/shard_map/ppermute | solution.py:25
  102.2 6.4 %collective-permute-start.9 = (f32[1,1024]{1,0:T(1,128)S(1)}, f32[1,1024]{1,0:T(1,128)S(1)}, u32[]{:S(2)}, u32[]{:S(2)}) collective-permute-start(f32[1,1024]{1,0:T(1,128)S(1)} %get-tuple-element.198), channel_id=1, source_target_pairs={{0,1},{1,2},{2,3},{3,4},{4,5},{5,6},{6,7},{7,8},{8,9},{9,10},{10,1... | collective-permute-start | bytes 12296 | tf_op jit(solution)/shard_map/ppermute | solution.py:24
  109.8 23.7 %all-to-all-start.2 = ((f32[16,1,256]{2,1,0:T(1,128)}), f32[16,1,256]{2,1,0:T(1,128)S(1)}, u32[]{:S(2)}, u32[]{:S(2)}) async-start(f32[16,1,256]{2,1,0:T(1,128)} %broadcast_in_dim.241), calls=%async_computation.2 | async-start | bytes 32768 | tf_op jit(solution)/shard_map/all_to_all | solution.py:32
  134.8 5.9 %collective-permute-start.10 = (f32[1,1024]{1,0:T(1,128)S(1)}, f32[1,1024]{1,0:T(1,128)S(1)}, u32[]{:S(2)}, u32[]{:S(2)}) collective-permute-start(f32[1,1024]{1,0:T(1,128)S(1)} %get-tuple-element.191), channel_id=1, source_target_pairs={{1,0},{2,1},{3,2},{4,3},{5,4},{6,5},{7,6},{8,7},{9,8},{10,9},{11,1... | collective-permute-start | bytes 12296 | tf_op jit(solution)/shard_map/ppermute | solution.py:25
  138.1 6.4 %collective-permute-start.11 = (f32[1,1024]{1,0:T(1,128)S(1)}, f32[1,1024]{1,0:T(1,128)S(1)}, u32[]{:S(2)}, u32[]{:S(2)}) collective-permute-start(f32[1,1024]{1,0:T(1,128)S(1)} %get-tuple-element.192), channel_id=1, source_target_pairs={{0,1},{1,2},{2,3},{3,4},{4,5},{5,6},{6,7},{7,8},{8,9},{9,10},{10,1... | collective-permute-start | bytes 12296 | tf_op jit(solution)/shard_map/ppermute | solution.py:24
  152.9 6.0 %collective-permute-start.12 = (f32[1,4096]{1,0:T(1,128)S(1)}, f32[1,4096]{1,0:T(1,128)S(1)}, u32[]{:S(2)}, u32[]{:S(2)}) collective-permute-start(f32[1,4096]{1,0:T(1,128)S(1)} %get-tuple-element.137), channel_id=1, source_target_pairs={{1,0},{2,1},{3,2},{4,3},{5,4},{6,5},{7,6},{8,7},{9,8},{10,9},{11,1... | collective-permute-start | bytes 49160 | tf_op jit(solution)/shard_map/ppermute | solution.py:25
  155.4 6.5 %collective-permute-start.13 = (f32[1,4096]{1,0:T(1,128)S(1)}, f32[1,4096]{1,0:T(1,128)S(1)}, u32[]{:S(2)}, u32[]{:S(2)}) collective-permute-start(f32[1,4096]{1,0:T(1,128)S(1)} %get-tuple-element.138), channel_id=1, source_target_pairs={{0,1},{1,2},{2,3},{3,4},{4,5},{5,6},{6,7},{7,8},{8,9},{9,10},{10,1... | collective-permute-start | bytes 49160 | tf_op jit(solution)/shard_map/ppermute | solution.py:24
  162.2 6.0 %collective-permute-start.14 = (f32[1,4096]{1,0:T(1,128)S(1)}, f32[1,4096]{1,0:T(1,128)S(1)}, u32[]{:S(2)}, u32[]{:S(2)}) collective-permute-start(f32[1,4096]{1,0:T(1,128)S(1)} %get-tuple-element.131), channel_id=1, source_target_pairs={{1,0},{2,1},{3,2},{4,3},{5,4},{6,5},{7,6},{8,7},{9,8},{10,9},{11,1... | collective-permute-start | bytes 49160 | tf_op jit(solution)/shard_map/ppermute | solution.py:25
  164.1 6.5 %collective-permute-start.15 = (f32[1,4096]{1,0:T(1,128)S(1)}, f32[1,4096]{1,0:T(1,128)S(1)}, u32[]{:S(2)}, u32[]{:S(2)}) collective-permute-start(f32[1,4096]{1,0:T(1,128)S(1)} %get-tuple-element.132), channel_id=1, source_target_pairs={{0,1},{1,2},{2,3},{3,4},{4,5},{5,6},{6,7},{7,8},{8,9},{9,10},{10,1... | collective-permute-start | bytes 49160 | tf_op jit(solution)/shard_map/ppermute | solution.py:24
  171.0 6.2 %collective-permute-start.16 = (f32[1,4096]{1,0:T(1,128)S(1)}, f32[1,4096]{1,0:T(1,128)S(1)}, u32[]{:S(2)}, u32[]{:S(2)}) collective-permute-start(f32[1,4096]{1,0:T(1,128)S(1)} %get-tuple-element.125), channel_id=1, source_target_pairs={{1,0},{2,1},{3,2},{4,3},{5,4},{6,5},{7,6},{8,7},{9,8},{10,9},{11,1... | collective-permute-start | bytes 49160 | tf_op jit(solution)/shard_map/ppermute | solution.py:25
  172.9 6.5 %collective-permute-start.17 = (f32[1,4096]{1,0:T(1,128)S(1)}, f32[1,4096]{1,0:T(1,128)S(1)}, u32[]{:S(2)}, u32[]{:S(2)}) collective-permute-start(f32[1,4096]{1,0:T(1,128)S(1)} %get-tuple-element.126), channel_id=1, source_target_pairs={{0,1},{1,2},{2,3},{3,4},{4,5},{5,6},{6,7},{7,8},{8,9},{9,10},{10,1... | collective-permute-start | bytes 49160 | tf_op jit(solution)/shard_map/ppermute | solution.py:24
  188.7 5.9 %collective-permute-start.18 = (f32[1,1024]{1,0:T(1,128)S(1)}, f32[1,1024]{1,0:T(1,128)S(1)}, u32[]{:S(2)}, u32[]{:S(2)}) collective-permute-start(f32[1,1024]{1,0:T(1,128)S(1)} %get-tuple-element.185), channel_id=1, source_target_pairs={{1,0},{2,1},{3,2},{4,3},{5,4},{6,5},{7,6},{8,7},{9,8},{10,9},{11,1... | collective-permute-start | bytes 12296 | tf_op jit(solution)/shard_map/ppermute | solution.py:25
  190.6 6.4 %collective-permute-start.19 = (f32[1,1024]{1,0:T(1,128)S(1)}, f32[1,1024]{1,0:T(1,128)S(1)}, u32[]{:S(2)}, u32[]{:S(2)}) collective-permute-start(f32[1,1024]{1,0:T(1,128)S(1)} %get-tuple-element.186), channel_id=1, source_target_pairs={{0,1},{1,2},{2,3},{3,4},{4,5},{5,6},{6,7},{7,8},{8,9},{9,10},{10,1... | collective-permute-start | bytes 12296 | tf_op jit(solution)/shard_map/ppermute | solution.py:24
  216.0 5.9 %collective-permute-start.20 = (f32[1,1024]{1,0:T(1,128)S(1)}, f32[1,1024]{1,0:T(1,128)S(1)}, u32[]{:S(2)}, u32[]{:S(2)}) collective-permute-start(f32[1,1024]{1,0:T(1,128)S(1)} %get-tuple-element.179), channel_id=1, source_target_pairs={{1,0},{2,1},{3,2},{4,3},{5,4},{6,5},{7,6},{8,7},{9,8},{10,9},{11,1... | collective-permute-start | bytes 12296 | tf_op jit(solution)/shard_map/ppermute | solution.py:25
  219.4 6.4 %collective-permute-start.21 = (f32[1,1024]{1,0:T(1,128)S(1)}, f32[1,1024]{1,0:T(1,128)S(1)}, u32[]{:S(2)}, u32[]{:S(2)}) collective-permute-start(f32[1,1024]{1,0:T(1,128)S(1)} %get-tuple-element.180), channel_id=1, source_target_pairs={{0,1},{1,2},{2,3},{3,4},{4,5},{5,6},{6,7},{7,8},{8,9},{9,10},{10,1... | collective-permute-start | bytes 12296 | tf_op jit(solution)/shard_map/ppermute | solution.py:24
  234.2 6.0 %collective-permute-start.22 = (f32[1,4096]{1,0:T(1,128)S(1)}, f32[1,4096]{1,0:T(1,128)S(1)}, u32[]{:S(2)}, u32[]{:S(2)}) collective-permute-start(f32[1,4096]{1,0:T(1,128)S(1)} %get-tuple-element.119), channel_id=1, source_target_pairs={{1,0},{2,1},{3,2},{4,3},{5,4},{6,5},{7,6},{8,7},{9,8},{10,9},{11,1... | collective-permute-start | bytes 49160 | tf_op jit(solution)/shard_map/ppermute | solution.py:25
  236.6 6.5 %collective-permute-start.23 = (f32[1,4096]{1,0:T(1,128)S(1)}, f32[1,4096]{1,0:T(1,128)S(1)}, u32[]{:S(2)}, u32[]{:S(2)}) collective-permute-start(f32[1,4096]{1,0:T(1,128)S(1)} %get-tuple-element.120), channel_id=1, source_target_pairs={{0,1},{1,2},{2,3},{3,4},{4,5},{5,6},{6,7},{7,8},{8,9},{9,10},{10,1... | collective-permute-start | bytes 49160 | tf_op jit(solution)/shard_map/ppermute | solution.py:24
where the time goes:
time: 245 us; the launch traced here: 244 us
  starting transfers between devices  108 us (44%)
  waiting for transfers between devices  52 us (21%)
  local copies, waits for them, and re-layouts  42.7 us (17%)
  blocking collectives  17.2 us (7%)
  other arithmetic  15.8 us (6%)
  matrix products  6.47 us (3%)
    ppermute x12, starting transfers between devices, extended(): before = lax.ppermute(last, axis, up)  41 us
    ppermute x12, waiting for transfers between devices, extended(): before = lax.ppermute(last, axis, up)  32.8 us
    ppermute x12, starting transfers between devices, extended(): after = lax.ppermute(leading, axis, down)  30.4 us
    all_to_all x2, starting transfers between devices, sent_to_all(): lax.all_to_all(jnp.broadcast_to(array[None], (length, *array.shape)), axi...  26.1 us
    all_to_all x2, waiting for transfers between devices, sent_to_all(): lax.all_to_all(jnp.broadcast_to(array[None], (length, *array.shape)), axi...  17.7 us
    all_to_all x1, blocking collectives, sent_to_all(): lax.all_to_all(jnp.broadcast_to(array[None], (length, *array.shape)), axi...  17.2 us
    reshape x2, local copies, waits for them, and re-layouts, restrict(): blocks = residual.reshape(planes // 2, 2, half_cells, 2, half_cells, 2)  12.7 us
    reshape x2, local copies, waits for them, and re-layouts, prolong(): return spread.reshape(2 * planes, 4 * half_cells * half_cells)  10.9 us
  transfers between devices with their start and end apart: 27, of which 14 were waited for; matrix products, arithmetic and copies ran while one was open for 5% of the time, Pallas kernels for 0%

commit v1 on v0

v1 whole, which is shorter than its diff:
```python
import functools

import jax
import jax.numpy as jnp
from jax import lax
from jax.experimental import pallas as pl
from jax.experimental.pallas import tpu as pltpu
from jax.sharding import PartitionSpec as P

MESH = pl.DeviceIdType.MESH
HIGHEST = lax.Precision.HIGHEST
NX = 64
OCC_DEN = 8
OMEGA = 0.8
COUPLING = 4.0
STEP = OMEGA / 6.0
GAIN0, GAIN1, GAIN2 = STEP, 4.0 * STEP, 16.0 * STEP


def iota(shape, axis):
    return lax.broadcasted_iota(jnp.int32, shape, axis)


def fine_cross(v):
    shape = v.shape
    lane, row = iota(shape, 2), iota(shape, 1)
    column = lane & 63
    west = jnp.where(column == 0, 0.0, pltpu.roll(v, 1, 2))
    east = jnp.where(column == 63, 0.0, pltpu.roll(v, 127, 2))
    odd = lane >= 64
    before = jnp.where(row == 0, 0.0, pltpu.roll(v, 1, 1))
    after = jnp.where(row == 31, 0.0, pltpu.roll(v, 31, 1))
    return west + east + pltpu.roll(v + jnp.where(odd, before, after), 64, 2)


def mid_cross(v):
    shape = v.shape
    lane, row = iota(shape, 2), iota(shape, 1)
    along = pltpu.roll(v, 1, 2) + pltpu.roll(v, 127, 2)
    before = jnp.where(row == 0, 0.0, pltpu.roll(v, 1, 1))
    after = jnp.where(row == 31, 0.0, pltpu.roll(v, 31, 1))
    return jnp.where(lane < 32, along + before + after, 0.0)


def relax(v, cross):
    inner = v[1:-1]
    return (1.0 - OMEGA) * inner + STEP * (cross(inner) + v[2:] + v[:-2])


def inside(v, first, planes):
    plane = iota(v.shape, 0) + first
    return jnp.where((plane >= 0) & (plane < planes), v, 0.0)


def flat_dot(v, m):
    n = v.shape[0]
    out = jnp.dot(v.reshape(n * v.shape[1], 128), m, precision=HIGHEST, preferred_element_type=jnp.float32)
    return out.reshape(n, v.shape[1], 128)


def restrict_fine(v):
    n = v.shape[0]
    pairs = v.reshape(n // 2, 2, 32, 128)
    lane, x = iota((128, 128), 0), iota((128, 128), 1)
    average = jnp.where(((lane & 63) >> 1) == x, 0.125, 0.0)
    return flat_dot(pairs[:, 0] + pairs[:, 1], average)


def prolong_fine(v):
    n = v.shape[0]
    x, lane = iota((128, 128), 0), iota((128, 128), 1)
    spread = flat_dot(v, jnp.where(((lane & 63) >> 1) == x, 1.0, 0.0))
    return jnp.broadcast_to(spread[:, None], (n, 2, 32, 128)).reshape(2 * n, 32, 128)


def own_group(shape):
    return ((iota(shape, len(shape) - 2) >> 1) & 7) == (iota(shape, len(shape) - 1) >> 4)


def restrict_mid(pair):
    x, lane = iota((128, 128), 0), iota((128, 128), 1)
    average = jnp.where(((lane & 15) == (x >> 1)) & (x < 32), 0.125, 0.0)
    both = jnp.dot(pair[0] + pair[1], average, precision=HIGHEST, preferred_element_type=jnp.float32)
    both = jnp.where(own_group(both.shape), both, 0.0)
    upper = jnp.sum(both[:16], axis=0, keepdims=True)
    lower = jnp.sum(both[16:], axis=0, keepdims=True)
    row = iota((8, 128), 0)
    return jnp.where(row == 0, upper, jnp.where(row == 1, lower, 0.0))


def prolong_mid(v):
    n = v.shape[0]
    rows = jnp.concatenate(
        [jnp.broadcast_to(v[:, 0:1], (n, 16, 128)), jnp.broadcast_to(v[:, 1:2], (n, 16, 128))], axis=1
    )
    rows = jnp.where(own_group(rows.shape), rows, 0.0)
    lane, x = iota((128, 128), 0), iota((128, 128), 1)
    spread = flat_dot(rows, jnp.where(((lane & 15) == (x >> 1)) & (x < 32), 1.0, 0.0))
    return jnp.broadcast_to(spread[:, None], (n, 2, 32, 128)).reshape(2 * n, 32, 128)


def coarse_solve(source):
    shape = source.shape
    lane, row = iota(shape, 2), iota(shape, 1)
    column, group = lane & 15, lane >> 4
    zero = jnp.zeros((1, *shape[1:]), jnp.float32)
    gained = GAIN2 * source
    v = gained
    for unused in range(3):
        west = jnp.where(column == 0, 0.0, pltpu.roll(v, 1, 2))
        east = jnp.where(column == 15, 0.0, pltpu.roll(v, 127, 2))
        back, on = pltpu.roll(v, 16, 2), pltpu.roll(v, 112, 2)
        before = jnp.where(group == 0, pltpu.roll(back, 1, 1), back)
        after = jnp.where(group == 7, pltpu.roll(on, 7, 1), on)
        plane = jnp.where(row < 2, west + east + before + after, 0.0)
        below = jnp.concatenate([zero, v[:-1]], axis=0)
        above = jnp.concatenate([v[1:], zero], axis=0)
        v = (1.0 - OMEGA) * v + STEP * (plane + below + above) + gained
    return v


def kernel(
    blocks, slabs,
    orb_ref, occ_ref, count_ref, ion_ref,
    pot_ref, kin_ref,
    dens, dens_in, field, field_below, field_above, rims, kin, kin_in,
    mids, coarse, coarse_again, padded, fine,
    send_sem, recv_sem,
):
    me, slab = lax.axis_index("cuts"), lax.axis_index("slab")
    planes = 4 * slabs

    def cut_at(r):
        return {"cuts": lax.rem(me + r, blocks)}

    def slab_at(r):
        return {"slab": lax.rem(slab + r + slabs, slabs)}

    barrier = pltpu.get_barrier_semaphore()

    @pl.loop(1, blocks)
    def _(r):
        pl.semaphore_signal(barrier, inc=1, device_id=cut_at(r), device_id_type=MESH)

    @pl.loop(1, slabs)
    def _(r):
        pl.semaphore_signal(barrier, inc=1, device_id=slab_at(r), device_id_type=MESH)

    def copy(stage, src, dst, device):
        return pltpu.make_async_remote_copy(
            src_ref=src, dst_ref=dst, send_sem=send_sem.at[stage], recv_sem=recv_sem.at[stage],
            device_id=device, device_id_type=MESH,
        )

    square = (32, 32)
    column = jnp.sum(
        jnp.where(
            iota(square, 0) == iota(square, 1),
            jnp.broadcast_to(occ_ref[...].astype(jnp.float32), square), 0.0,
        ),
        axis=1, keepdims=True,
    ) * (1.0 / OCC_DEN)
    live = iota((32, 128), 0) < count_ref[0]
    weight = jnp.where(live, jnp.broadcast_to(column, (32, 128)), 0.0)

    def tile(z, c):
        return orb_ref[z, :, pl.ds(pl.multiple_of(c * 128, 128), 128)].astype(jnp.float32)

    @pl.loop(0, blocks)
    def _(c):
        rows = []
        for z in range(4):
            p = tile(z, c)
            rows.append(jnp.sum(weight * (p * p), axis=0, keepdims=True))
        dens[c] = jnp.concatenate(rows, axis=0)

    pl.semaphore_wait(barrier, blocks + slabs - 2)

    @pl.loop(1, blocks)
    def _(r):
        copy(0, dens.at[lax.rem(me + r, blocks)], dens_in.at[r], cut_at(r)).start()

    up, down = slab_at(1), slab_at(-1)
    rim_up = copy(1, orb_ref.at[3], rims.at[0], up)
    rim_down = copy(2, orb_ref.at[0], rims.at[1], down)
    rim_up.start()
    rim_down.start()
    dens_in[0] = dens[me]

    lane = iota((32, 128), 1)
    x = lane & 63
    odd = lane >= 64

    @pl.loop(0, blocks)
    def _(c):
        left = jnp.where(c > 0, 1.0, 0.0)
        right = jnp.where(c < blocks - 1, 1.0, 0.0)
        ps = [tile(z, c) for z in range(4)]
        rows = []
        for z in range(4):
            p = ps[z]
            along = jnp.where(x == 0, 0.0, p) - jnp.where(x == 1, 0.0, pltpu.roll(p, 2, 1))
            total = pltpu.roll(weight * (along * along), 127, 1)
            back = p - left * tile(z, lax.max(c - 1, 0))
            on = right * tile(z, lax.min(c + 1, blocks - 1)) - p
            across = jnp.where(odd, back, on)
            total += pltpu.roll(weight * (across * across), 64, 1)
            if z in (1, 2):
                steep = ps[z + 1] - ps[z - 1]
                total += weight * (steep * steep)
            rows.append(jnp.sum(total, axis=0, keepdims=True) * 0.125)
        kin[c] = jnp.concatenate(rows, axis=0)

    copy(0, dens_in.at[pl.ds(1, blocks - 1)], dens_in.at[pl.ds(1, blocks - 1)], cut_at(1)).wait_recv()
    charge = ion_ref[:, pl.ds(pl.multiple_of(me * 128, 128), 128)]
    field[me] = COUPLING * (jnp.sum(dens_in[...], axis=0) - charge)

    @pl.loop(1, blocks)
    def _(r):
        copy(3, field.at[me], field.at[me], cut_at(r)).start()

    gathered = field.at[pl.ds(0, blocks - 1)]
    copy(3, gathered, gathered, cut_at(1)).wait_recv()
    field_up = copy(4, field, field_below, up)
    field_down = copy(5, field, field_above, down)
    field_up.start()
    field_down.start()
    field_up.wait_recv()
    field_down.wait_recv()

    for z in range(3):
        fine[z] = field_below[:, z + 1, :]
        fine[z + 7] = field_above[:, z, :]
    for z in range(4):
        fine[z + 3] = field[:, z, :]
    first = 4 * slab
    forcing = inside(fine[...], first - 3, planes)
    left1 = inside(relax(forcing, fine_cross), first - 2, planes)
    left2 = inside(relax(left1, fine_cross), first - 1, planes)
    left3 = relax(left2, fine_cross)
    direct = GAIN0 * (forcing[3:7] + left1[2:6] + left2[1:5] + left3)
    source = restrict_fine(left1)
    again = restrict_fine(left3)
    mids[3] = (
        source[1] + pltpu.roll(source[2], 32, 1) + pltpu.roll(again[0], 64, 1) + pltpu.roll(again[1], 96, 1)
    )
    coarse[slab] = restrict_mid(relax(source, mid_cross))
    for away in (1, -1, 2, -2, 3, -3):
        copy(6, mids.at[3], mids.at[3 - away], slab_at(away)).start()

    @pl.loop(1, slabs)
    def _(r):
        copy(7, coarse.at[slab], coarse.at[slab], slab_at(r)).start()

    rim_up.wait_recv()
    rim_down.wait_recv()
    has_below = jnp.where(slab > 0, 1.0, 0.0)
    has_above = jnp.where(slab < slabs - 1, 1.0, 0.0)
    row4 = iota((4, 128), 0)

    @pl.loop(0, blocks)
    def _(c):
        at = pl.ds(pl.multiple_of(c * 128, 128), 128)
        low = tile(1, c) - has_below * rims[0, :, at].astype(jnp.float32)
        high = has_above * rims[1, :, at].astype(jnp.float32) - tile(2, c)
        low = jnp.sum(weight * (low * low), axis=0, keepdims=True) * 0.125
        high = jnp.sum(weight * (high * high), axis=0, keepdims=True) * 0.125
        kin[c] += jnp.where(row4 == 0, low, jnp.where(row4 == 3, high, 0.0))

    @pl.loop(1, blocks)
    def _(r):
        copy(8, kin.at[lax.rem(me + r, blocks)], kin_in.at[r], cut_at(r)).start()

    kin_in[0] = kin[me]

    all_but_one = coarse.at[pl.ds(0, slabs - 1)]
    copy(7, all_but_one, all_but_one, up).wait_recv()
    padded[pl.ds(0, 3)] = jnp.zeros((3, 8, 128), jnp.float32)
    padded[pl.ds(slabs + 3, 3)] = jnp.zeros((3, 8, 128), jnp.float32)
    padded[pl.ds(3, slabs)] = coarse_solve(coarse[...])
    lifted = prolong_mid(padded[pl.ds(slab, 7)])
    copy(6, mids.at[pl.ds(0, 6)], mids.at[pl.ds(0, 6)], up).wait_recv()
    near = mids[...]
    use = iota((7, 32, 128), 2) < 32
    even = jnp.where(use, near, 0.0)
    uneven = jnp.where(use, pltpu.roll(near, 96, 2), 0.0)
    even_again = jnp.where(use, pltpu.roll(near, 64, 2), 0.0)[2:5]
    uneven_again = jnp.where(use, pltpu.roll(near, 32, 2), 0.0)[2:5]
    mid = 2 * slab
    source = jnp.concatenate([even[:, None], uneven[:, None]], axis=1).reshape(14, 32, 128)
    source = inside(source, mid - 6, 2 * slabs)
    again = jnp.concatenate([even_again[:, None], uneven_again[:, None]], axis=1).reshape(6, 32, 128)
    guess = GAIN1 * source[1:13] + lifted[1:13]
    error = inside(relax(guess, mid_cross) + GAIN1 * source[2:12], mid - 4, 2 * slabs)
    spread = prolong_fine(error)[1:19]
    back1 = inside(relax(spread, fine_cross), first - 6, planes)
    back2 = inside(relax(back1, fine_cross), first - 5, planes)
    back3 = relax(back2, fine_cross)
    direct += back3[4:8]
    source = again - restrict_fine((back2[1:13] - back3) * (1.0 / GAIN0))
    source = inside(source, mid - 2, 2 * slabs)

    coarse_again[slab] = restrict_mid(relax(source[1:5], mid_cross))

    @pl.loop(1, slabs)
    def _(r):
        copy(9, coarse_again.at[slab], coarse_again.at[slab], slab_at(r)).start()

    all_but_one = coarse_again.at[pl.ds(0, slabs - 1)]
    copy(9, all_but_one, all_but_one, up).wait_recv()
    padded[pl.ds(3, slabs)] = coarse_solve(coarse_again[...])
    lifted = prolong_mid(padded[pl.ds(slab + 2, 3)])
    guess = GAIN1 * source + lifted
    error = inside(relax(guess, mid_cross) + GAIN1 * source[1:5], mid - 1, 2 * slabs)
    pot_ref[...] = direct + relax(prolong_fine(error)[1:7], fine_cross)

    copy(8, kin_in.at[pl.ds(1, blocks - 1)], kin_in.at[pl.ds(1, blocks - 1)], cut_at(1)).wait_recv()
    kin_ref[...] = jnp.sum(kin_in[...], axis=0)

    copy(0, dens_in.at[pl.ds(1, blocks - 1)], dens_in.at[pl.ds(1, blocks - 1)], cut_at(1)).wait_send()
    rim_up.wait_send()
    rim_down.wait_send()
    copy(3, gathered, gathered, cut_at(1)).wait_send()
    field_up.wait_send()
    field_down.wait_send()
    copy(6, mids.at[pl.ds(0, 6)], mids.at[pl.ds(0, 6)], up).wait_send()
    copy(7, all_but_one, all_but_one, up).wait_send()
    copy(8, kin_in.at[pl.ds(1, blocks - 1)], kin_in.at[pl.ds(1, blocks - 1)], cut_at(1)).wait_send()
    copy(9, all_but_one, all_but_one, up).wait_send()


def solution(mesh):
    blocks, slabs = mesh.shape["cuts"], mesh.shape["slab"]

    def shards(orbitals, occupation, state_counts, ion_charge):
        f32 = jnp.float32
        by_plane = jnp.transpose(orbitals, (1, 0, 2))
        vmem = pl.BlockSpec(memory_space=pltpu.VMEM)
        smem = pl.BlockSpec(memory_space=pltpu.SMEM)
        potential, kinetic = pl.pallas_call(
            functools.partial(kernel, blocks, slabs),
            out_shape=(jax.ShapeDtypeStruct((4, 32, 128), f32), jax.ShapeDtypeStruct((4, 128), f32)),
            in_specs=[vmem, vmem, smem, vmem],
            out_specs=(vmem, vmem),
            scratch_shapes=[
                pltpu.VMEM((blocks, 4, 128), f32),
                pltpu.VMEM((blocks, 4, 128), f32),
                pltpu.VMEM((blocks, 4, 128), f32),
                pltpu.VMEM((blocks, 4, 128), f32),
                pltpu.VMEM((blocks, 4, 128), f32),
                pltpu.VMEM((2, 32, 4096), jnp.bfloat16),
                pltpu.VMEM((blocks, 4, 128), f32),
                pltpu.VMEM((blocks, 4, 128), f32),
                pltpu.VMEM((7, 32, 128), f32),
                pltpu.VMEM((slabs, 8, 128), f32),
                pltpu.VMEM((slabs, 8, 128), f32),
                pltpu.VMEM((slabs + 6, 8, 128), f32),
                pltpu.VMEM((10, 32, 128), f32),
                pltpu.SemaphoreType.DMA((10,)),
                pltpu.SemaphoreType.DMA((10,)),
            ],
            compiler_params=pltpu.CompilerParams(collective_id=0, has_side_effects=True),
        )(by_plane, occupation, state_counts, ion_charge)
        return potential.reshape(4, 4096), kinetic

    return jax.shard_map(
        shards,
        mesh=mesh,
        in_specs=(P("cuts", "slab", None), P("cuts", None), P("cuts"), P("slab", None)),
        out_specs=(P("slab", None), P("slab", "cuts")),
        check_vma=False,
    )
```

time: 245 us -> 58.8 us (0.24)
  the two profiles are of different devices: /device:TPU:64 before, /device:TPU:1 now
where the time goes in v1:
time: 58.8 us; the launch traced here: 57.9 us
  Pallas kernels  51.7 us (88%)
  local copies, waits for them, and re-layouts  4.88 us (8%)
  between operations  1.29 us (2%)
    pallas_call x1, Pallas kernels, shards(): pl.pallas_call(functools.partial(kernel, blocks, slabs), out_shape=(jax.S...  51.7 us
    unnamed x5, local copies, waits for them, and re-layouts  4.88 us

profile of v1, /device:TPU:1, one launch (start us, length us, event | category | flops | bytes accessed | tf_op | source)
XLA Modules:
  0.0 57.9 jit_solution(11965908596001909618)
XLA Ops:
  1.3 2.8 %copy.10 = bf16[32,4,4096]{2,0,1:T(8,128)(2,1)} copy(bf16[32,4,4096]{2,1,0:T(4,128)(2,1)} %param.4) | data formatting | bytes 2097152 | tf_op args[0]
  4.1 51.7 %shard_map.59 = (f32[4,32,128]{2,1,0:T(8,128)}, f32[4,128]{1,0:T(4,128)}) custom-call(bf16[4,32,4096]{2,1,0:T(8,128)(2,1)} %bitcast.7, s32[1,32]{1,0:T(1,128)} %occ_ref.1, s32[1]{0:T(128)S(6)} %copy.13.count_ref, f32[4,4096]{1,0:T(4,128)} %ion_ref.1), custom_call_target="tpu_custom_call" | custom-call | tf_op jit(solution)/shard_map/pallas_call | solution.py:340
  55.8 0.0 copy-start
  55.8 1.5 %copy.11 = f32[1,4,32,128]{3,1,2,0:T(4,128)} copy(f32[1,4,32,128]{3,2,1,0:T(8,128)} %bitcast.9) | data formatting | bytes 131072
  57.3 0.0 copy-done
  57.3 0.6 copy.14
Async XLA Ops:
  55.8 1.5 %copy-start = (f32[4,128]{1,0:T(4,128)S(1)}, f32[4,128]{1,0:T(4,128)}, u32[]{:S(2)}) copy-start(f32[4,128]{1,0:T(4,128)} %get-tuple-element.9) | copy-start | bytes 6148

commit v2 on v1

v2 whole, which is shorter than its diff:
```python
import functools

import jax
import jax.numpy as jnp
from jax import lax
from jax.experimental import pallas as pl
from jax.experimental.pallas import tpu as pltpu
from jax.sharding import PartitionSpec as P

MESH = pl.DeviceIdType.MESH
HIGHEST = lax.Precision.HIGHEST
NX = 64
OCC_DEN = 8
OMEGA = 0.8
COUPLING = 4.0
STEP = OMEGA / 6.0
GAIN0, GAIN1, GAIN2 = STEP, 4.0 * STEP, 16.0 * STEP


def iota(shape, axis):
    return lax.broadcasted_iota(jnp.int32, shape, axis)


def fine_cross(v):
    shape = v.shape
    lane, row = iota(shape, 2), iota(shape, 1)
    column = lane & 63
    west = jnp.where(column == 0, 0.0, pltpu.roll(v, 1, 2))
    east = jnp.where(column == 63, 0.0, pltpu.roll(v, 127, 2))
    odd = lane >= 64
    before = jnp.where(row == 0, 0.0, pltpu.roll(v, 1, 1))
    after = jnp.where(row == 31, 0.0, pltpu.roll(v, 31, 1))
    return west + east + pltpu.roll(v + jnp.where(odd, before, after), 64, 2)


def mid_cross(v):
    shape = v.shape
    lane, row = iota(shape, 2), iota(shape, 1)
    along = pltpu.roll(v, 1, 2) + pltpu.roll(v, 127, 2)
    before = jnp.where(row == 0, 0.0, pltpu.roll(v, 1, 1))
    after = jnp.where(row == 31, 0.0, pltpu.roll(v, 31, 1))
    return jnp.where(lane < 32, along + before + after, 0.0)


def relax(v, cross):
    inner = v[1:-1]
    return (1.0 - OMEGA) * inner + STEP * (cross(inner) + v[2:] + v[:-2])


def grow(v, cross):
    n = v.shape[0]
    none = jnp.zeros((1, *v.shape[1:]), jnp.float32)
    both = jnp.concatenate([none, none], axis=0)
    middle = jnp.concatenate([none, (1.0 - OMEGA) * v + STEP * cross(v), none], axis=0)
    return middle + STEP * (jnp.concatenate([both, v], axis=0) + jnp.concatenate([v, both], axis=0))


def widened(v, n):
    none = jnp.zeros((n, *v.shape[1:]), jnp.float32)
    return jnp.concatenate([none, v, none], axis=0)


def packed(planes):
    return sum(pltpu.roll(p, 32 * k, 1) if k else p for k, p in enumerate(planes))


def group(v, k):
    return pltpu.roll(v, (128 - 32 * k) % 128, v.ndim - 1) if k else v


def woven(even, odd):
    n = even.shape[0]
    v = jnp.concatenate([even[:, None], odd[:, None]], axis=1).reshape(2 * n, 32, 128)
    return jnp.where(iota(v.shape, 2) < 32, v, 0.0)


def inside(v, first, planes):
    plane = iota(v.shape, 0) + first
    return jnp.where((plane >= 0) & (plane < planes), v, 0.0)


def flat_dot(v, m):
    n = v.shape[0]
    out = jnp.dot(v.reshape(n * v.shape[1], 128), m, precision=HIGHEST, preferred_element_type=jnp.float32)
    return out.reshape(n, v.shape[1], 128)


def restrict_fine(v):
    n = v.shape[0]
    pairs = v.reshape(n // 2, 2, 32, 128)
    lane, x = iota((128, 128), 0), iota((128, 128), 1)
    average = jnp.where(((lane & 63) >> 1) == x, 0.125, 0.0)
    return flat_dot(pairs[:, 0] + pairs[:, 1], average)


def prolong_fine(v):
    n = v.shape[0]
    x, lane = iota((128, 128), 0), iota((128, 128), 1)
    spread = flat_dot(v, jnp.where(((lane & 63) >> 1) == x, 1.0, 0.0))
    return jnp.broadcast_to(spread[:, None], (n, 2, 32, 128)).reshape(2 * n, 32, 128)


def own_group(shape):
    return ((iota(shape, len(shape) - 2) >> 1) & 7) == (iota(shape, len(shape) - 1) >> 4)


def restrict_mid(low, high):
    x, lane = iota((128, 128), 0), iota((128, 128), 1)
    average = jnp.where(((lane & 15) == (x >> 1)) & (x < 32), 0.125, 0.0)
    both = jnp.dot(low + high, average, precision=HIGHEST, preferred_element_type=jnp.float32)
    both = jnp.where(own_group(both.shape), both, 0.0)
    return jnp.sum(both[:16], axis=0, keepdims=True), jnp.sum(both[16:], axis=0, keepdims=True)


def in_rows(rows):
    at = iota((8, 128), 0)
    tile = jnp.zeros((8, 128), jnp.float32)
    for k, row in enumerate(rows):
        tile = jnp.where(at == k, row, tile)
    return tile


def prolong_mid(v):
    n = v.shape[0]
    rows = jnp.concatenate(
        [jnp.broadcast_to(v[:, 0:1], (n, 16, 128)), jnp.broadcast_to(v[:, 1:2], (n, 16, 128))], axis=1
    )
    rows = jnp.where(own_group(rows.shape), rows, 0.0)
    lane, x = iota((128, 128), 0), iota((128, 128), 1)
    spread = flat_dot(rows, jnp.where(((lane & 15) == (x >> 1)) & (x < 32), 1.0, 0.0))
    return jnp.broadcast_to(spread[:, None], (n, 2, 32, 128)).reshape(2 * n, 32, 128)


def coarse_solve(source):
    shape = source.shape
    lane, row = iota(shape, 2), iota(shape, 1)
    column, group = lane & 15, lane >> 4
    zero = jnp.zeros((1, *shape[1:]), jnp.float32)
    gained = GAIN2 * source
    v = gained
    for unused in range(3):
        west = jnp.where(column == 0, 0.0, pltpu.roll(v, 1, 2))
        east = jnp.where(column == 15, 0.0, pltpu.roll(v, 127, 2))
        back, on = pltpu.roll(v, 16, 2), pltpu.roll(v, 112, 2)
        before = jnp.where(group == 0, pltpu.roll(back, 1, 1), back)
        after = jnp.where(group == 7, pltpu.roll(on, 7, 1), on)
        plane = jnp.where(row < 2, west + east + before + after, 0.0)
        below = jnp.concatenate([zero, v[:-1]], axis=0)
        above = jnp.concatenate([v[1:], zero], axis=0)
        v = (1.0 - OMEGA) * v + STEP * (plane + below + above) + gained
    return v


def kernel(
    blocks, slabs,
    orb_ref, occ_ref, count_ref, ion_ref,
    pot_ref, kin_ref,
    raw, wide, stage, planar, dens, dens_in, field, rims, kin, kin_in,
    near_f, near_g, near_h, spill, spill_in, coarse, coarse_again, padded, fine,
    load_sem, send_sem, recv_sem,
):
    me, slab = lax.axis_index("cuts"), lax.axis_index("slab")
    planes = 4 * slabs

    load = pltpu.make_async_copy(orb_ref, raw, load_sem)
    load.start()

    def cut_at(r):
        return {"cuts": lax.rem(me + r, blocks)}

    def slab_at(r):
        return {"slab": lax.rem(slab + r + slabs, slabs)}

    barrier = pltpu.get_barrier_semaphore()

    @pl.loop(1, blocks)
    def _(r):
        pl.semaphore_signal(barrier, inc=1, device_id=cut_at(r), device_id_type=MESH)

    @pl.loop(1, slabs)
    def _(r):
        pl.semaphore_signal(barrier, inc=1, device_id=slab_at(r), device_id_type=MESH)

    def copy(stage, src, dst, device):
        return pltpu.make_async_remote_copy(
            src_ref=src, dst_ref=dst, send_sem=send_sem.at[stage], recv_sem=recv_sem.at[stage],
            device_id=device, device_id_type=MESH,
        )

    def columns(c):
        return pl.ds(pl.multiple_of(c * 128, 128), 128)

    coarse_again[...] = jnp.zeros_like(coarse_again)
    square = (32, 32)
    column = jnp.sum(
        jnp.where(
            iota(square, 0) == iota(square, 1),
            jnp.broadcast_to(occ_ref[...].astype(jnp.float32), square), 0.0,
        ),
        axis=1, keepdims=True,
    ) * (1.0 / OCC_DEN)
    live = iota((32, 128), 0) < jnp.broadcast_to(count_ref[...], (32, 128))
    weight = jnp.where(live, jnp.broadcast_to(column, (32, 128)), 0.0)
    wide[...] = jnp.broadcast_to(weight[:, None], (32, 4, 128))
    load.wait()

    @pl.loop(0, blocks)
    def _(c):
        p = raw[:, :, columns(c)].astype(jnp.float32)
        dens[c] = jnp.sum(wide[...] * (p * p), axis=0)

    pl.semaphore_wait(barrier, blocks + slabs - 2)

    @pl.loop(1, blocks)
    def _(r):
        copy(0, dens.at[lax.rem(me + r, blocks)], dens_in.at[r], cut_at(r)).start()

    dens_in[0] = dens[me]

    @pl.loop(0, blocks)
    def _(c):
        stage[...] = raw[:, :, columns(c)].astype(jnp.float32).reshape(128, 128)
        for z in range(4):
            planar[z, :, columns(c)] = stage[pl.ds(z, 32, stride=4), :].astype(jnp.bfloat16)

    up, down = slab_at(1), slab_at(-1)
    rim_up = copy(1, planar.at[3], rims.at[0], up)
    rim_down = copy(2, planar.at[0], rims.at[1], down)
    rim_up.start()
    rim_down.start()

    copy(0, dens_in.at[pl.ds(1, blocks - 1)], dens_in.at[pl.ds(1, blocks - 1)], cut_at(1)).wait_recv()
    field[me] = COUPLING * (jnp.sum(dens_in[...], axis=0) - ion_ref[:, columns(me)])

    @pl.loop(1, blocks)
    def _(r):
        copy(3, field.at[me], field.at[me], cut_at(r)).start()

    lane = iota((32, 128), 1)
    x = lane & 63
    odd = lane >= 64

    def tile(z, c):
        return planar[z, :, columns(c)].astype(jnp.float32)

    def folded(v):
        return (v[:8] + v[8:16]) + (v[16:24] + v[24:])

    @pl.loop(0, blocks)
    def _(c):
        left = jnp.where(c > 0, 1.0, 0.0)
        right = jnp.where(c < blocks - 1, 1.0, 0.0)
        ps = [tile(z, c) for z in range(4)]
        rows = []
        for z in range(4):
            p = ps[z]
            along = jnp.where(x == 0, 0.0, p) - jnp.where(x == 1, 0.0, pltpu.roll(p, 2, 1))
            total = pltpu.roll(folded(weight * (along * along)), 127, 1)
            back = p - left * tile(z, lax.max(c - 1, 0))
            on = right * tile(z, lax.min(c + 1, blocks - 1)) - p
            across = jnp.where(odd, back, on)
            total += pltpu.roll(folded(weight * (across * across)), 64, 1)
            if z in (1, 2):
                steep = ps[z + 1] - ps[z - 1]
                total += folded(weight * (steep * steep))
            rows.append(jnp.sum(total, axis=0, keepdims=True) * 0.125)
        kin[c] = jnp.concatenate(rows, axis=0)

    gathered = field.at[pl.ds(0, blocks - 1)]
    copy(3, gathered, gathered, cut_at(1)).wait_recv()

    for z in range(4):
        fine[z] = field[:, z, :]
    first, mid = 4 * slab, 2 * slab
    forcing = fine[...]
    left1 = inside(grow(forcing, fine_cross), first - 1, planes)
    left2 = inside(grow(left1, fine_cross), first - 2, planes)
    left3 = inside(grow(left2, fine_cross), first - 3, planes)
    source = restrict_fine(widened(left1, 1))
    below = inside(grow(source, mid_cross), mid - 2, 2 * slabs)
    coarse[slab] = in_rows([row for k in range(3) for row in restrict_mid(below[2 * k], below[2 * k + 1])])

    @pl.loop(1, slabs)
    def _(r):
        copy(6, coarse.at[slab], coarse.at[slab], slab_at(r)).start()

    near_f[3] = packed([source[k] for k in range(4)])
    again = restrict_fine(widened(left3, 1))
    near_g[2] = packed([again[0], again[1], again[4], again[5]])
    near_h[1] = packed([again[2], again[3]])
    for away in (1, -1, 2, -2, 3, -3):
        copy(7, near_f.at[3], near_f.at[3 - away], slab_at(away)).start()
    for away in (1, -1, 2, -2):
        copy(8, near_g.at[2], near_g.at[2 - away], slab_at(away)).start()
    for away in (1, -1):
        copy(9, near_h.at[1], near_h.at[1 - away], slab_at(away)).start()
    direct = GAIN0 * (left3 + widened(left2, 1) + widened(left1, 2) + widened(forcing, 3))
    spill[0] = direct[:3]
    spill[1] = direct[7:]
    direct = direct[3:7]
    spill_up = copy(4, spill.at[1], spill_in.at[0], up)
    spill_down = copy(5, spill.at[0], spill_in.at[1], down)
    spill_up.start()
    spill_down.start()

    rim_up.wait_recv()
    rim_down.wait_recv()
    has_below = jnp.where(slab > 0, 1.0, 0.0)
    has_above = jnp.where(slab < slabs - 1, 1.0, 0.0)
    row4 = iota((4, 128), 0)

    @pl.loop(0, blocks)
    def _(c):
        low = tile(1, c) - has_below * rims[0, :, columns(c)].astype(jnp.float32)
        high = has_above * rims[1, :, columns(c)].astype(jnp.float32) - tile(2, c)
        low = jnp.sum(weight * (low * low), axis=0, keepdims=True) * 0.125
        high = jnp.sum(weight * (high * high), axis=0, keepdims=True) * 0.125
        kin[c] += jnp.where(row4 == 0, low, jnp.where(row4 == 3, high, 0.0))

    @pl.loop(1, blocks)
    def _(r):
        copy(10, kin.at[lax.rem(me + r, blocks)], kin_in.at[r], cut_at(r)).start()

    kin_in[0] = kin[me]

    all_but_one = coarse.at[pl.ds(0, slabs - 1)]
    copy(6, all_but_one, all_but_one, up).wait_recv()
    parts = coarse[...]
    none = jnp.zeros((1, 8, 128), jnp.float32)
    parts = (
        pltpu.roll(parts, 6, 1)
        + jnp.concatenate([none, pltpu.roll(parts, 4, 1)[:-1]], axis=0)
        + jnp.concatenate([parts[1:], none], axis=0)
    )
    padded[pl.ds(0, 3)] = jnp.zeros((3, 8, 128), jnp.float32)
    padded[pl.ds(slabs + 3, 3)] = jnp.zeros((3, 8, 128), jnp.float32)
    padded[pl.ds(3, slabs)] = coarse_solve(jnp.where(iota(parts.shape, 1) < 2, parts, 0.0))
    lifted = prolong_mid(padded[pl.ds(slab, 7)])
    copy(7, near_f.at[pl.ds(0, 6)], near_f.at[pl.ds(0, 6)], up).wait_recv()
    near = inside(near_f[...], slab - 3, slabs)
    none = jnp.zeros((1, 32, 128), jnp.float32)
    source = woven(
        group(near, 1) + jnp.concatenate([none, group(near, 3)[:-1]], axis=0),
        group(near, 2) + jnp.concatenate([near[1:], none], axis=0),
    )
    source = inside(source, mid - 6, 2 * slabs)
    guess = GAIN1 * source[1:13] + lifted[1:13]
    error = inside(relax(guess, mid_cross) + GAIN1 * source[2:12], mid - 4, 2 * slabs)
    spread = prolong_fine(error)[1:19]
    back1 = inside(relax(spread, fine_cross), first - 6, planes)
    back2 = inside(relax(back1, fine_cross), first - 5, planes)
    back3 = relax(back2, fine_cross)
    direct += back3[4:8]
    copy(8, near_g.at[pl.ds(0, 4)], near_g.at[pl.ds(0, 4)], up).wait_recv()
    copy(9, near_h.at[pl.ds(0, 2)], near_h.at[pl.ds(0, 2)], up).wait_recv()
    near, own = inside(near_g[...], slab - 2, slabs), near_h[...]
    again = woven(
        own + group(near, 2)[0:3] + near[2:5],
        group(own, 1) + group(near, 1)[2:5] + group(near, 3)[0:3],
    )
    source = again - restrict_fine((back2[1:13] - back3) * (1.0 / GAIN0))
    source = inside(source, mid - 2, 2 * slabs)

    smoothed = relax(source[1:5], mid_cross)
    coarse_again[slab] = in_rows(restrict_mid(smoothed[0], smoothed[1]))
    for away in (4, -4, 3, -3, 2, -2, 1, -1):
        copy(11, coarse_again.at[slab], coarse_again.at[slab], slab_at(away)).start()

    spill_up.wait_recv()
    spill_down.wait_recv()
    direct += jnp.concatenate([spill_in[0], none], axis=0) + jnp.concatenate([none, spill_in[1]], axis=0)
    some = coarse_again.at[pl.ds(0, 8)]
    copy(11, some, some, up).wait_recv()
    padded[pl.ds(3, slabs)] = coarse_solve(coarse_again[...])
    lifted = prolong_mid(padded[pl.ds(slab + 2, 3)])
    guess = GAIN1 * source + lifted
    error = inside(relax(guess, mid_cross) + GAIN1 * source[1:5], mid - 1, 2 * slabs)
    fine[...] = direct + relax(prolong_fine(error)[1:7], fine_cross)
    for c in range(blocks):
        pot_ref[:, c * 128 : (c + 1) * 128] = fine[:, c, :]

    copy(10, kin_in.at[pl.ds(1, blocks - 1)], kin_in.at[pl.ds(1, blocks - 1)], cut_at(1)).wait_recv()
    kin_ref[...] = jnp.sum(kin_in[...], axis=0)

    copy(0, dens_in.at[pl.ds(1, blocks - 1)], dens_in.at[pl.ds(1, blocks - 1)], cut_at(1)).wait_send()
    rim_up.wait_send()
    rim_down.wait_send()
    copy(3, gathered, gathered, cut_at(1)).wait_send()
    spill_up.wait_send()
    spill_down.wait_send()
    copy(6, all_but_one, all_but_one, up).wait_send()
    copy(7, near_f.at[pl.ds(0, 6)], near_f.at[pl.ds(0, 6)], up).wait_send()
    copy(8, near_g.at[pl.ds(0, 4)], near_g.at[pl.ds(0, 4)], up).wait_send()
    copy(9, near_h.at[pl.ds(0, 2)], near_h.at[pl.ds(0, 2)], up).wait_send()
    copy(10, kin_in.at[pl.ds(1, blocks - 1)], kin_in.at[pl.ds(1, blocks - 1)], cut_at(1)).wait_send()
    copy(11, some, some, up).wait_send()


def solution(mesh):
    blocks, slabs = mesh.shape["cuts"], mesh.shape["slab"]

    def shards(orbitals, occupation, state_counts, ion_charge):
        f32, bf16 = jnp.float32, jnp.bfloat16
        vmem = pl.BlockSpec(memory_space=pltpu.VMEM)
        return pl.pallas_call(
            functools.partial(kernel, blocks, slabs),
            out_shape=(jax.ShapeDtypeStruct((4, 4096), f32), jax.ShapeDtypeStruct((4, 128), f32)),
            in_specs=[pl.BlockSpec(memory_space=pl.ANY), vmem, vmem, vmem],
            out_specs=(vmem, vmem),
            scratch_shapes=[
                pltpu.VMEM((32, 4, 4096), bf16),
                pltpu.VMEM((32, 4, 128), f32),
                pltpu.VMEM((128, 128), f32),
                pltpu.VMEM((4, 32, 4096), bf16),
                pltpu.VMEM((blocks, 4, 128), f32),
                pltpu.VMEM((blocks, 4, 128), f32),
                pltpu.VMEM((blocks, 4, 128), f32),
                pltpu.VMEM((2, 32, 4096), bf16),
                pltpu.VMEM((blocks, 4, 128), f32),
                pltpu.VMEM((blocks, 4, 128), f32),
                pltpu.VMEM((7, 32, 128), f32),
                pltpu.VMEM((5, 32, 128), f32),
                pltpu.VMEM((3, 32, 128), f32),
                pltpu.VMEM((2, 3, 32, 128), f32),
                pltpu.VMEM((2, 3, 32, 128), f32),
                pltpu.VMEM((slabs, 8, 128), f32),
                pltpu.VMEM((slabs, 8, 128), f32),
                pltpu.VMEM((slabs + 6, 8, 128), f32),
                pltpu.VMEM((4, 32, 128), f32),
                pltpu.SemaphoreType.DMA,
                pltpu.SemaphoreType.DMA((12,)),
                pltpu.SemaphoreType.DMA((12,)),
            ],
            compiler_params=pltpu.CompilerParams(collective_id=0, has_side_effects=True),
        )(orbitals, occupation, state_counts.reshape(1, 1), ion_charge)

    return jax.shard_map(
        shards,
        mesh=mesh,
        in_specs=(P("cuts", "slab", None), P("cuts", None), P("cuts"), P("slab", None)),
        out_specs=(P("slab", None), P("slab", "cuts")),
        check_vma=False,
    )
```

time: 58.8 us -> 50.1 us (0.85); the launches traced: 57.9 us -> 49.9 us
  Pallas kernels: 51.7 us -> 46.5 us
  local copies, waits for them, and re-layouts: 4.88 us -> 2.06 us
    pallas_call x1, Pallas kernels: 51.7 us -> 46.5 us  [shards(): pl.pallas_call(functools.partial(kernel, blocks, slabs), out_shape=(jax.S...]
    unnamed x5 -> x4, local copies, waits for them, and re-layouts: 4.88 us -> 2.06 us
where the time goes in v2:
time: 50.1 us; the launch traced here: 49.9 us
  Pallas kernels  46.5 us (93%)
  local copies, waits for them, and re-layouts  2.06 us (4%)
  between operations  1.29 us (3%)
    pallas_call x1, Pallas kernels, shards(): pl.pallas_call(functools.partial(kernel, blocks, slabs), out_shape=(jax.S...  46.5 us
    unnamed x4, local copies, waits for them, and re-layouts  2.06 us

profile of v2, /device:TPU:1, one launch (start us, length us, event | category | flops | bytes accessed | tf_op | source)
XLA Modules:
  0.0 49.9 jit_solution(3363435174769386687)
XLA Ops:
  1.3 46.5 %shard_map.59 = (f32[4,4096]{1,0:T(4,128)}, f32[4,128]{1,0:T(4,128)}) custom-call(bf16[32,4,4096]{2,1,0:T(4,128)(2,1)} %orb_ref.1, s32[1,32]{1,0:T(1,128)} %occ_ref.1, s32[1,1]{1,0:T(1,128)} %bitcast.1.count_ref, f32[4,4096]{1,0:T(4,128)} %ion_ref.1), custom_call_target="tpu_custom_call" | custom-call | tf_op jit(solution)/shard_map/pallas_call | solution.py:405
  47.8 0.0 copy-start
  47.8 1.5 %copy.9 = f32[4,4096]{1,0:T(4,128)} copy(f32[4,4096]{1,0:T(4,128)} %get-tuple-element.4) | data formatting | bytes 131072
  49.3 0.0 copy-done
  49.3 0.6 %copy.10 = f32[4,128]{1,0:T(4,128)} copy(f32[4,128]{1,0:T(4,128)S(1)} %copy-done) | data formatting | bytes 4096
Async XLA Ops:
  47.8 1.5 %copy-start = (f32[4,128]{1,0:T(4,128)S(1)}, f32[4,128]{1,0:T(4,128)}, u32[]{:S(2)}) copy-start(f32[4,128]{1,0:T(4,128)} %get-tuple-element.5) | copy-start | bytes 6148

commit v3 on v2

--- a/solution.py
+++ b/solution.py
@@ -151,6 +151,10 @@
     return v
 
 
+def far_first(n):
+    return sorted(range(n), key=lambda step: -min(step, n - step))
+
+
 def kernel(
     blocks, slabs,
     orb_ref, occ_ref, count_ref, ion_ref,
@@ -165,21 +169,28 @@
     load = pltpu.make_async_copy(orb_ref, raw, load_sem)
     load.start()
 
-    def cut_at(r):
-        return {"cuts": lax.rem(me + r, blocks)}
+    ring = blocks // 4
+    half, y, core = me // (2 * ring), lax.rem(me // 2, ring), lax.rem(me, 2)
+    others = [
+        (h * ring + lax.rem(y + step, ring)) * 2 + c
+        for step in far_first(ring)
+        for h in (1 - half, half)
+        for c in (1 - core, core)
+    ][:-1]
+
+    def cut_at(number):
+        return {"cuts": number}
 
     def slab_at(r):
         return {"slab": lax.rem(slab + r + slabs, slabs)}
 
+    other_slabs = [slab_at(step) for step in far_first(slabs)[:-1]]
+
+    up, down, down_cut = slab_at(1), slab_at(-1), cut_at(others[-1])
     barrier = pltpu.get_barrier_semaphore()
 
-    @pl.loop(1, blocks)
-    def _(r):
-        pl.semaphore_signal(barrier, inc=1, device_id=cut_at(r), device_id_type=MESH)
-
-    @pl.loop(1, slabs)
-    def _(r):
-        pl.semaphore_signal(barrier, inc=1, device_id=slab_at(r), device_id_type=MESH)
+    for device in [cut_at(number) for number in others] + other_slabs:
+        pl.semaphore_signal(barrier, inc=1, device_id=device, device_id_type=MESH)
 
     def copy(stage, src, dst, device):
         return pltpu.make_async_remote_copy(
@@ -199,7 +210,7 @@
         ),
         axis=1, keepdims=True,
     ) * (1.0 / OCC_DEN)
-    live = iota((32, 128), 0) < jnp.broadcast_to(count_ref[...], (32, 128))
+    live = iota((32, 128), 0) < count_ref[0]
     weight = jnp.where(live, jnp.broadcast_to(column, (32, 128)), 0.0)
     wide[...] = jnp.broadcast_to(weight[:, None], (32, 4, 128))
     load.wait()
@@ -211,11 +222,10 @@
 
     pl.semaphore_wait(barrier, blocks + slabs - 2)
 
-    @pl.loop(1, blocks)
-    def _(r):
-        copy(0, dens.at[lax.rem(me + r, blocks)], dens_in.at[r], cut_at(r)).start()
-
-    dens_in[0] = dens[me]
+    for k, number in enumerate(others):
+        copy(0, dens.at[number], dens_in.at[k], cut_at(number)).start()
+
+    dens_in[blocks - 1] = dens[me]
 
     @pl.loop(0, blocks)
     def _(c):
@@ -223,18 +233,15 @@
         for z in range(4):
             planar[z, :, columns(c)] = stage[pl.ds(z, 32, stride=4), :].astype(jnp.bfloat16)
 
-    up, down = slab_at(1), slab_at(-1)
-    rim_up = copy(1, planar.at[3], rims.at[0], up)
-    rim_down = copy(2, planar.at[0], rims.at[1], down)
-    rim_up.start()
-    rim_down.start()
-
-    copy(0, dens_in.at[pl.ds(1, blocks - 1)], dens_in.at[pl.ds(1, blocks - 1)], cut_at(1)).wait_recv()
-    field[me] = COUPLING * (jnp.sum(dens_in[...], axis=0) - ion_ref[:, columns(me)])
-
-    @pl.loop(1, blocks)
-    def _(r):
-        copy(3, field.at[me], field.at[me], cut_at(r)).start()
+    def rim_copies(k):
+        states = pl.ds(16 * k, 16)
+        return (
+            copy(1 + k, planar.at[3, states], rims.at[0, states], up),
+            copy(12 + k, planar.at[0, states], rims.at[1, states], down),
+        )
+
+    for rim in rim_copies(0):
+        rim.start()
 
     lane = iota((32, 128), 1)
     x = lane & 63
@@ -246,8 +253,7 @@
     def folded(v):
         return (v[:8] + v[8:16]) + (v[16:24] + v[24:])
 
-    @pl.loop(0, blocks)
-    def _(c):
+    def plain_terms(c):
         left = jnp.where(c > 0, 1.0, 0.0)
         right = jnp.where(c < blocks - 1, 1.0, 0.0)
         ps = [tile(z, c) for z in range(4)]
@@ -266,30 +272,43 @@
             rows.append(jnp.sum(total, axis=0, keepdims=True) * 0.125)
         kin[c] = jnp.concatenate(rows, axis=0)
 
+    early = 3 * blocks // 8
+    pl.loop(0, early)(plain_terms)
+
+    copy(0, dens_in.at[pl.ds(0, blocks - 1)], dens_in.at[pl.ds(0, blocks - 1)], down_cut).wait_recv()
+    field[me] = COUPLING * (jnp.sum(dens_in[...], axis=0) - ion_ref[:, columns(me)])
+
+    for number in others:
+        copy(3, field.at[me], field.at[me], cut_at(number)).start()
+
+    for rim in rim_copies(1):
+        rim.start()
+
+    pl.loop(early, blocks)(plain_terms)
+
     gathered = field.at[pl.ds(0, blocks - 1)]
-    copy(3, gathered, gathered, cut_at(1)).wait_recv()
+    copy(3, gathered, gathered, down_cut).wait_recv()
 
     for z in range(4):
         fine[z] = field[:, z, :]
     first, mid = 4 * slab, 2 * slab
     forcing = fine[...]
     left1 = inside(grow(forcing, fine_cross), first - 1, planes)
-    left2 = inside(grow(left1, fine_cross), first - 2, planes)
-    left3 = inside(grow(left2, fine_cross), first - 3, planes)
     source = restrict_fine(widened(left1, 1))
     below = inside(grow(source, mid_cross), mid - 2, 2 * slabs)
     coarse[slab] = in_rows([row for k in range(3) for row in restrict_mid(below[2 * k], below[2 * k + 1])])
 
-    @pl.loop(1, slabs)
-    def _(r):
-        copy(6, coarse.at[slab], coarse.at[slab], slab_at(r)).start()
+    for device in other_slabs:
+        copy(6, coarse.at[slab], coarse.at[slab], device).start()
 
     near_f[3] = packed([source[k] for k in range(4)])
+    for away in (1, -1, 2, -2, 3, -3):
+        copy(7, near_f.at[3], near_f.at[3 - away], slab_at(away)).start()
+    left2 = inside(grow(left1, fine_cross), first - 2, planes)
+    left3 = inside(grow(left2, fine_cross), first - 3, planes)
     again = restrict_fine(widened(left3, 1))
     near_g[2] = packed([again[0], again[1], again[4], again[5]])
     near_h[1] = packed([again[2], again[3]])
-    for away in (1, -1, 2, -2, 3, -3):
-        copy(7, near_f.at[3], near_f.at[3 - away], slab_at(away)).start()
     for away in (1, -1, 2, -2):
         copy(8, near_g.at[2], near_g.at[2 - away], slab_at(away)).start()
     for away in (1, -1):
@@ -303,8 +322,9 @@
     spill_up.start()
     spill_down.start()
 
-    rim_up.wait_recv()
-    rim_down.wait_recv()
+    for k in range(2):
+        for rim in rim_copies(k):
+            rim.wait_recv()
     has_below = jnp.where(slab > 0, 1.0, 0.0)
     has_above = jnp.where(slab < slabs - 1, 1.0, 0.0)
     row4 = iota((4, 128), 0)
@@ -317,11 +337,10 @@
         high = jnp.sum(weight * (high * high), axis=0, keepdims=True) * 0.125
         kin[c] += jnp.where(row4 == 0, low, jnp.where(row4 == 3, high, 0.0))
 
-    @pl.loop(1, blocks)
-    def _(r):
-        copy(10, kin.at[lax.rem(me + r, blocks)], kin_in.at[r], cut_at(r)).start()
-
-    kin_in[0] = kin[me]
+    for k, number in enumerate(others):
+        copy(10, kin.at[number], kin_in.at[k], cut_at(number)).start()
+
+    kin_in[blocks - 1] = kin[me]
 
     all_but_one = coarse.at[pl.ds(0, slabs - 1)]
     copy(6, all_but_one, all_but_one, up).wait_recv()
@@ -379,20 +398,21 @@
     for c in range(blocks):
         pot_ref[:, c * 128 : (c + 1) * 128] = fine[:, c, :]
 
-    copy(10, kin_in.at[pl.ds(1, blocks - 1)], kin_in.at[pl.ds(1, blocks - 1)], cut_at(1)).wait_recv()
+    copy(10, kin_in.at[pl.ds(0, blocks - 1)], kin_in.at[pl.ds(0, blocks - 1)], down_cut).wait_recv()
     kin_ref[...] = jnp.sum(kin_in[...], axis=0)
 
-    copy(0, dens_in.at[pl.ds(1, blocks - 1)], dens_in.at[pl.ds(1, blocks - 1)], cut_at(1)).wait_send()
-    rim_up.wait_send()
-    rim_down.wait_send()
-    copy(3, gathered, gathered, cut_at(1)).wait_send()
+    copy(0, dens_in.at[pl.ds(0, blocks - 1)], dens_in.at[pl.ds(0, blocks - 1)], down_cut).wait_send()
+    for k in range(2):
+        for rim in rim_copies(k):
+            rim.wait_send()
+    copy(3, gathered, gathered, down_cut).wait_send()
     spill_up.wait_send()
     spill_down.wait_send()
     copy(6, all_but_one, all_but_one, up).wait_send()
     copy(7, near_f.at[pl.ds(0, 6)], near_f.at[pl.ds(0, 6)], up).wait_send()
     copy(8, near_g.at[pl.ds(0, 4)], near_g.at[pl.ds(0, 4)], up).wait_send()
     copy(9, near_h.at[pl.ds(0, 2)], near_h.at[pl.ds(0, 2)], up).wait_send()
-    copy(10, kin_in.at[pl.ds(1, blocks - 1)], kin_in.at[pl.ds(1, blocks - 1)], cut_at(1)).wait_send()
+    copy(10, kin_in.at[pl.ds(0, blocks - 1)], kin_in.at[pl.ds(0, blocks - 1)], down_cut).wait_send()
     copy(11, some, some, up).wait_send()
 
 
@@ -401,11 +421,11 @@
 
     def shards(orbitals, occupation, state_counts, ion_charge):
         f32, bf16 = jnp.float32, jnp.bfloat16
-        vmem = pl.BlockSpec(memory_space=pltpu.VMEM)
+        vmem, smem = pl.BlockSpec(memory_space=pltpu.VMEM), pl.BlockSpec(memory_space=pltpu.SMEM)
         return pl.pallas_call(
             functools.partial(kernel, blocks, slabs),
             out_shape=(jax.ShapeDtypeStruct((4, 4096), f32), jax.ShapeDtypeStruct((4, 128), f32)),
-            in_specs=[pl.BlockSpec(memory_space=pl.ANY), vmem, vmem, vmem],
+            in_specs=[pl.BlockSpec(memory_space=pl.ANY), vmem, smem, vmem],
             out_specs=(vmem, vmem),
             scratch_shapes=[
                 pltpu.VMEM((32, 4, 4096), bf16),
@@ -428,11 +448,11 @@
                 pltpu.VMEM((slabs + 6, 8, 128), f32),
                 pltpu.VMEM((4, 32, 128), f32),
                 pltpu.SemaphoreType.DMA,
-                pltpu.SemaphoreType.DMA((12,)),
-                pltpu.SemaphoreType.DMA((12,)),
+                pltpu.SemaphoreType.DMA((14,)),
+                pltpu.SemaphoreType.DMA((14,)),
             ],
-            compiler_params=pltpu.CompilerParams(collective_id=0, has_side_effects=True),
-        )(orbitals, occupation, state_counts.reshape(1, 1), ion_charge)
+            compiler_params=pltpu.CompilerParams(collective_id=0, has_side_effects=True, vmem_limit_bytes=55_930_000),
+        )(orbitals, occupation, state_counts, ion_charge)
 
     return jax.shard_map(
         shards,

time: 50.1 us -> 47.3 us (0.944)
  the two profiles are of different devices: /device:TPU:1 before, /device:TPU:8 now
where the time goes in v3:
time: 47.3 us; the launch traced here: 47.1 us
  Pallas kernels  43.7 us (92%)
  local copies, waits for them, and re-layouts  2.05 us (4%)
  between operations  1.32 us (3%)
    pallas_call x1, Pallas kernels, shards(): pl.pallas_call(functools.partial(kernel, blocks, slabs), out_shape=(jax.S...  43.7 us
    unnamed x6, local copies, waits for them, and re-layouts  2.05 us

profile of v3, /device:TPU:8, one launch (start us, length us, event | category | flops | bytes accessed | tf_op | source)
XLA Modules:
  0.0 47.1 jit_solution(4159596456435300451)
XLA Ops:
  0.6 0.0 copy-start.1
  1.3 0.0 copy-done.1
  1.3 0.0 copy-start
  1.3 0.8 %copy-done = f32[4,4096]{1,0:T(4,128)S(1)} copy-done((f32[4,4096]{1,0:T(4,128)S(1)}, f32[4,4096]{1,0:T(4,128)}, u32[]{:S(2)}) %copy-start) | copy-done | bytes 65560
  2.1 43.7 %shard_map.59 = (f32[4,4096]{1,0:T(4,128)S(1)}, f32[4,128]{1,0:T(4,128)S(1)}) custom-call(bf16[32,4,4096]{2,1,0:T(4,128)(2,1)} %orb_ref.1, s32[1,32]{1,0:T(1,128)S(1)} %copy-done.1, s32[1]{0:T(128)S(6)} %copy.8.count_ref, f32[4,4096]{1,0:T(4,128)S(1)} %copy-done), custom_call_target="tpu_custom_call" | custom-call | tf_op jit(solution)/shard_map/pallas_call | solution.py:425
  45.9 0.6 %copy.9 = f32[4,4096]{1,0:T(4,128)} copy(f32[4,4096]{1,0:T(4,128)S(1)} %get-tuple-element.4) | data formatting | bytes 131072
  46.5 0.6 %copy.10 = f32[4,128]{1,0:T(4,128)} copy(f32[4,128]{1,0:T(4,128)S(1)} %get-tuple-element.5) | data formatting | bytes 4096
Async XLA Ops:
  0.6 0.7 %copy-start.1 = (s32[1,32]{1,0:T(1,128)S(1)}, s32[1,32]{1,0:T(1,128)}, u32[]{:S(2)}) copy-start(s32[1,32]{1,0:T(1,128)} %occ_ref.1) | copy-start | bytes 388
  1.3 0.8 %copy-start = (f32[4,4096]{1,0:T(4,128)S(1)}, f32[4,4096]{1,0:T(4,128)}, u32[]{:S(2)}) copy-start(f32[4,4096]{1,0:T(4,128)} %ion_ref.1) | copy-start | bytes 196612

commit v4 on v3

--- a/solution.py
+++ b/solution.py
@@ -8,7 +8,6 @@
 from jax.sharding import PartitionSpec as P
 
 MESH = pl.DeviceIdType.MESH
-HIGHEST = lax.Precision.HIGHEST
 NX = 64
 OCC_DEN = 8
 OMEGA = 0.8
@@ -79,10 +78,20 @@
     return jnp.where((plane >= 0) & (plane < planes), v, 0.0)
 
 
+def exact_dot(v, m):
+    m = m.astype(jnp.bfloat16)
+    total = None
+    for unused in range(3):
+        part = v.astype(jnp.bfloat16)
+        v = v - part.astype(jnp.float32)
+        term = jnp.dot(part, m, preferred_element_type=jnp.float32)
+        total = term if total is None else total + term
+    return total
+
+
 def flat_dot(v, m):
     n = v.shape[0]
-    out = jnp.dot(v.reshape(n * v.shape[1], 128), m, precision=HIGHEST, preferred_element_type=jnp.float32)
-    return out.reshape(n, v.shape[1], 128)
+    return exact_dot(v.reshape(n * v.shape[1], 128), m).reshape(n, v.shape[1], 128)
 
 
 def restrict_fine(v):
@@ -107,7 +116,7 @@
 def restrict_mid(low, high):
     x, lane = iota((128, 128), 0), iota((128, 128), 1)
     average = jnp.where(((lane & 15) == (x >> 1)) & (x < 32), 0.125, 0.0)
-    both = jnp.dot(low + high, average, precision=HIGHEST, preferred_element_type=jnp.float32)
+    both = exact_dot(low + high, average)
     both = jnp.where(own_group(both.shape), both, 0.0)
     return jnp.sum(both[:16], axis=0, keepdims=True), jnp.sum(both[16:], axis=0, keepdims=True)
 
@@ -159,15 +168,19 @@
     blocks, slabs,
     orb_ref, occ_ref, count_ref, ion_ref,
     pot_ref, kin_ref,
-    raw, wide, stage, planar, dens, dens_in, field, rims, kin, kin_in,
-    near_f, near_g, near_h, spill, spill_in, coarse, coarse_again, padded, fine,
+    occ, ion, raw, wide, stage, planar, dens, dens_in, field, rims, kin, kin_in,
+    near, low_near, own_near, spill, spill_in, coarse, coarse_again, padded, fine,
     load_sem, send_sem, recv_sem,
 ):
     me, slab = lax.axis_index("cuts"), lax.axis_index("slab")
     planes = 4 * slabs
 
-    load = pltpu.make_async_copy(orb_ref, raw, load_sem)
+    load = pltpu.make_async_copy(orb_ref, raw, load_sem.at[0])
+    load_small = pltpu.make_async_copy(occ_ref, occ, load_sem.at[1])
+    load_ion = pltpu.make_async_copy(ion_ref, ion, load_sem.at[2])
+    load_small.start()
     load.start()
+    load_ion.start()
 
     ring = blocks // 4
     half, y, core = me // (2 * ring), lax.rem(me // 2, ring), lax.rem(me, 2)
@@ -202,11 +215,12 @@
         return pl.ds(pl.multiple_of(c * 128, 128), 128)
 
     coarse_again[...] = jnp.zeros_like(coarse_again)
+    load_small.wait()
     square = (32, 32)
     column = jnp.sum(
         jnp.where(
             iota(square, 0) == iota(square, 1),
-            jnp.broadcast_to(occ_ref[...].astype(jnp.float32), square), 0.0,
+            jnp.broadcast_to(occ[...].astype(jnp.float32), square), 0.0,
         ),
         axis=1, keepdims=True,
     ) * (1.0 / OCC_DEN)
@@ -234,10 +248,10 @@
             planar[z, :, columns(c)] = stage[pl.ds(z, 32, stride=4), :].astype(jnp.bfloat16)
 
     def rim_copies(k):
-        states = pl.ds(16 * k, 16)
+        part = pl.ds(2048 * k, 2048)
         return (
-            copy(1 + k, planar.at[3, states], rims.at[0, states], up),
-            copy(12 + k, planar.at[0, states], rims.at[1, states], down),
+            copy(1 + k, planar.at[3, :, part], rims.at[0, :, part], up),
+            copy(12 + k, planar.at[0, :, part], rims.at[1, :, part], down),
         )
 
     for rim in rim_copies(0):
@@ -276,7 +290,8 @@
     pl.loop(0, early)(plain_terms)
 
     copy(0, dens_in.at[pl.ds(0, blocks - 1)], dens_in.at[pl.ds(0, blocks - 1)], down_cut).wait_recv()
-    field[me] = COUPLING * (jnp.sum(dens_in[...], axis=0) - ion_ref[:, columns(me)])
+    load_ion.wait()
+    field[me] = COUPLING * (jnp.sum(dens_in[...], axis=0) - ion[:, columns(me)])
 
     for number in others:
         copy(3, field.at[me], field.at[me], cut_at(number)).start()
@@ -295,32 +310,30 @@
     forcing = fine[...]
     left1 = inside(grow(forcing, fine_cross), first - 1, planes)
     source = restrict_fine(widened(left1, 1))
+    near[6] = packed([source[k] for k in range(4)])
+    for k, away in enumerate((3, -3, 2, -2, 1, -1)):
+        copy(7, near.at[6], near.at[k], slab_at(away)).start()
     below = inside(grow(source, mid_cross), mid - 2, 2 * slabs)
     coarse[slab] = in_rows([row for k in range(3) for row in restrict_mid(below[2 * k], below[2 * k + 1])])
 
     for device in other_slabs:
         copy(6, coarse.at[slab], coarse.at[slab], device).start()
 
-    near_f[3] = packed([source[k] for k in range(4)])
-    for away in (1, -1, 2, -2, 3, -3):
-        copy(7, near_f.at[3], near_f.at[3 - away], slab_at(away)).start()
     left2 = inside(grow(left1, fine_cross), first - 2, planes)
     left3 = inside(grow(left2, fine_cross), first - 3, planes)
     again = restrict_fine(widened(left3, 1))
-    near_g[2] = packed([again[0], again[1], again[4], again[5]])
-    near_h[1] = packed([again[2], again[3]])
-    for away in (1, -1, 2, -2):
-        copy(8, near_g.at[2], near_g.at[2 - away], slab_at(away)).start()
-    for away in (1, -1):
-        copy(9, near_h.at[1], near_h.at[1 - away], slab_at(away)).start()
+    own_near[0] = packed([again[0], again[1], again[4], again[5]])
+    own_near[1] = packed([again[2], again[3]])
+    toward = 1 - 2 * core
+    for k, (block, steps) in enumerate(((0, 1), (0, 2), (1, 1))):
+        copy(8, own_near.at[block], low_near.at[core, k], slab_at(steps * toward)).start()
     direct = GAIN0 * (left3 + widened(left2, 1) + widened(left1, 2) + widened(forcing, 3))
     spill[0] = direct[:3]
     spill[1] = direct[7:]
     direct = direct[3:7]
-    spill_up = copy(4, spill.at[1], spill_in.at[0], up)
-    spill_down = copy(5, spill.at[0], spill_in.at[1], down)
-    spill_up.start()
-    spill_down.start()
+    spill_over = copy(4, spill.at[1 - core], spill_in.at[core], slab_at(toward))
+    spill_over.start()
+    spill_pass = copy(5, spill_in.at[core], spill_in.at[core], down_cut)
 
     for k in range(2):
         for rim in rim_copies(k):
@@ -355,12 +368,17 @@
     padded[pl.ds(slabs + 3, 3)] = jnp.zeros((3, 8, 128), jnp.float32)
     padded[pl.ds(3, slabs)] = coarse_solve(jnp.where(iota(parts.shape, 1) < 2, parts, 0.0))
     lifted = prolong_mid(padded[pl.ds(slab, 7)])
-    copy(7, near_f.at[pl.ds(0, 6)], near_f.at[pl.ds(0, 6)], up).wait_recv()
-    near = inside(near_f[...], slab - 3, slabs)
+    copy(7, near.at[pl.ds(0, 6)], near.at[pl.ds(0, 6)], up).wait_recv()
+    arrived = low_near.at[core]
+    copy(8, arrived, arrived, down_cut).wait_recv()
+    near_pass = copy(9, arrived, arrived, down_cut)
+    near_pass.start()
+    near_f = jnp.stack([near[0], near[2], near[4], near[6], near[5], near[3], near[1]])
+    near_f = inside(near_f, slab - 3, slabs)
     none = jnp.zeros((1, 32, 128), jnp.float32)
     source = woven(
-        group(near, 1) + jnp.concatenate([none, group(near, 3)[:-1]], axis=0),
-        group(near, 2) + jnp.concatenate([near[1:], none], axis=0),
+        group(near_f, 1) + jnp.concatenate([none, group(near_f, 3)[:-1]], axis=0),
+        group(near_f, 2) + jnp.concatenate([near_f[1:], none], axis=0),
     )
     source = inside(source, mid - 6, 2 * slabs)
     guess = GAIN1 * source[1:13] + lifted[1:13]
@@ -370,12 +388,13 @@
     back2 = inside(relax(back1, fine_cross), first - 5, planes)
     back3 = relax(back2, fine_cross)
     direct += back3[4:8]
-    copy(8, near_g.at[pl.ds(0, 4)], near_g.at[pl.ds(0, 4)], up).wait_recv()
-    copy(9, near_h.at[pl.ds(0, 2)], near_h.at[pl.ds(0, 2)], up).wait_recv()
-    near, own = inside(near_g[...], slab - 2, slabs), near_h[...]
+    near_pass.wait_recv()
+    near_g = jnp.stack([low_near[0, 1], low_near[0, 0], own_near[0], low_near[1, 0], low_near[1, 1]])
+    near_g = inside(near_g, slab - 2, slabs)
+    near_h = jnp.stack([low_near[0, 2], own_near[1], low_near[1, 2]])
     again = woven(
-        own + group(near, 2)[0:3] + near[2:5],
-        group(own, 1) + group(near, 1)[2:5] + group(near, 3)[0:3],
+        near_h + group(near_g, 2)[0:3] + near_g[2:5],
+        group(near_h, 1) + group(near_g, 1)[2:5] + group(near_g, 3)[0:3],
     )
     source = again - restrict_fine((back2[1:13] - back3) * (1.0 / GAIN0))
     source = inside(source, mid - 2, 2 * slabs)
@@ -385,11 +404,12 @@
     for away in (4, -4, 3, -3, 2, -2, 1, -1):
         copy(11, coarse_again.at[slab], coarse_again.at[slab], slab_at(away)).start()
 
-    spill_up.wait_recv()
-    spill_down.wait_recv()
-    direct += jnp.concatenate([spill_in[0], none], axis=0) + jnp.concatenate([none, spill_in[1]], axis=0)
+    spill_over.wait_recv()
+    spill_pass.start()
     some = coarse_again.at[pl.ds(0, 8)]
     copy(11, some, some, up).wait_recv()
+    spill_pass.wait_recv()
+    direct += jnp.concatenate([spill_in[0], none], axis=0) + jnp.concatenate([none, spill_in[1]], axis=0)
     padded[pl.ds(3, slabs)] = coarse_solve(coarse_again[...])
     lifted = prolong_mid(padded[pl.ds(slab + 2, 3)])
     guess = GAIN1 * source + lifted
@@ -406,12 +426,12 @@
         for rim in rim_copies(k):
             rim.wait_send()
     copy(3, gathered, gathered, down_cut).wait_send()
-    spill_up.wait_send()
-    spill_down.wait_send()
+    spill_over.wait_send()
+    spill_pass.wait_send()
     copy(6, all_but_one, all_but_one, up).wait_send()
-    copy(7, near_f.at[pl.ds(0, 6)], near_f.at[pl.ds(0, 6)], up).wait_send()
-    copy(8, near_g.at[pl.ds(0, 4)], near_g.at[pl.ds(0, 4)], up).wait_send()
-    copy(9, near_h.at[pl.ds(0, 2)], near_h.at[pl.ds(0, 2)], up).wait_send()
+    copy(7, near.at[pl.ds(0, 6)], near.at[pl.ds(0, 6)], up).wait_send()
+    copy(8, arrived, arrived, down_cut).wait_send()
+    near_pass.wait_send()
     copy(10, kin_in.at[pl.ds(0, blocks - 1)], kin_in.at[pl.ds(0, blocks - 1)], down_cut).wait_send()
     copy(11, some, some, up).wait_send()
 
@@ -421,13 +441,15 @@
 
     def shards(orbitals, occupation, state_counts, ion_charge):
         f32, bf16 = jnp.float32, jnp.bfloat16
-        vmem, smem = pl.BlockSpec(memory_space=pltpu.VMEM), pl.BlockSpec(memory_space=pltpu.SMEM)
+        anywhere, vmem = pl.BlockSpec(memory_space=pl.ANY), pl.BlockSpec(memory_space=pltpu.VMEM)
         return pl.pallas_call(
             functools.partial(kernel, blocks, slabs),
             out_shape=(jax.ShapeDtypeStruct((4, 4096), f32), jax.ShapeDtypeStruct((4, 128), f32)),
-            in_specs=[pl.BlockSpec(memory_space=pl.ANY), vmem, smem, vmem],
+            in_specs=[anywhere, anywhere, pl.BlockSpec(memory_space=pltpu.SMEM), anywhere],
             out_specs=(vmem, vmem),
             scratch_shapes=[
+                pltpu.VMEM((1, 32), jnp.int32),
+                pltpu.VMEM((4, 4096), f32),
                 pltpu.VMEM((32, 4, 4096), bf16),
                 pltpu.VMEM((32, 4, 128), f32),
                 pltpu.VMEM((128, 128), f32),
@@ -439,19 +461,19 @@
                 pltpu.VMEM((blocks, 4, 128), f32),
                 pltpu.VMEM((blocks, 4, 128), f32),
                 pltpu.VMEM((7, 32, 128), f32),
-                pltpu.VMEM((5, 32, 128), f32),
-                pltpu.VMEM((3, 32, 128), f32),
+                pltpu.VMEM((2, 3, 32, 128), f32),
+                pltpu.VMEM((2, 32, 128), f32),
                 pltpu.VMEM((2, 3, 32, 128), f32),
                 pltpu.VMEM((2, 3, 32, 128), f32),
                 pltpu.VMEM((slabs, 8, 128), f32),
                 pltpu.VMEM((slabs, 8, 128), f32),
                 pltpu.VMEM((slabs + 6, 8, 128), f32),
                 pltpu.VMEM((4, 32, 128), f32),
-                pltpu.SemaphoreType.DMA,
+                pltpu.SemaphoreType.DMA((3,)),
                 pltpu.SemaphoreType.DMA((14,)),
                 pltpu.SemaphoreType.DMA((14,)),
             ],
-            compiler_params=pltpu.CompilerParams(collective_id=0, has_side_effects=True, vmem_limit_bytes=55_930_000),
+            compiler_params=pltpu.CompilerParams(collective_id=0, has_side_effects=True, vmem_limit_bytes=55_900_000),
         )(orbitals, occupation, state_counts, ion_charge)
 
     return jax.shard_map(

time: 47.3 us -> 46.3 us (0.979)
  the two profiles are of different devices: /device:TPU:8 before, /device:TPU:1 now
where the time goes in v4:
time: 46.3 us; the launch traced here: 46.1 us
  Pallas kernels  42.8 us (92%)
  local copies, waits for them, and re-layouts  2.05 us (4%)
  between operations  1.32 us (3%)
    pallas_call x1, Pallas kernels, shards(): pl.pallas_call(functools.partial(kernel, blocks, slabs), out_shape=(jax.S...  42.8 us
    unnamed x6, local copies, waits for them, and re-layouts  2.05 us

profile of v4, /device:TPU:1, one launch (start us, length us, event | category | flops | bytes accessed | tf_op | source)
XLA Modules:
  0.0 46.1 jit_solution(16275229358336640195)
XLA Ops:
  0.6 0.0 copy-start.1
  1.3 0.0 copy-done.1
  1.3 0.0 copy-start
  1.3 0.8 %copy-done = f32[4,4096]{1,0:T(4,128)S(1)} copy-done((f32[4,4096]{1,0:T(4,128)S(1)}, f32[4,4096]{1,0:T(4,128)}, u32[]{:S(2)}) %copy-start) | copy-done | bytes 65560
  2.1 42.8 %shard_map.59 = (f32[4,4096]{1,0:T(4,128)S(1)}, f32[4,128]{1,0:T(4,128)S(1)}) custom-call(bf16[32,4,4096]{2,1,0:T(4,128)(2,1)} %orb_ref.1, s32[1,32]{1,0:T(1,128)S(1)} %copy-done.1, s32[1]{0:T(128)S(6)} %copy.8.count_ref, f32[4,4096]{1,0:T(4,128)S(1)} %copy-done), custom_call_target="tpu_custom_call" | custom-call | tf_op jit(solution)/shard_map/pallas_call | solution.py:445
  44.9 0.6 %copy.9 = f32[4,4096]{1,0:T(4,128)} copy(f32[4,4096]{1,0:T(4,128)S(1)} %get-tuple-element.4) | data formatting | bytes 131072
  45.5 0.6 %copy.10 = f32[4,128]{1,0:T(4,128)} copy(f32[4,128]{1,0:T(4,128)S(1)} %get-tuple-element.5) | data formatting | bytes 4096
Async XLA Ops:
  0.6 0.7 %copy-start.1 = (s32[1,32]{1,0:T(1,128)S(1)}, s32[1,32]{1,0:T(1,128)}, u32[]{:S(2)}) copy-start(s32[1,32]{1,0:T(1,128)} %occ_ref.1) | copy-start | bytes 388
  1.3 0.8 %copy-start = (f32[4,4096]{1,0:T(4,128)S(1)}, f32[4,4096]{1,0:T(4,128)}, u32[]{:S(2)}) copy-start(f32[4,4096]{1,0:T(4,128)} %ion_ref.1) | copy-start | bytes 196612

commit v5 on v4

--- a/solution.py
+++ b/solution.py
@@ -357,6 +357,10 @@
 
     all_but_one = coarse.at[pl.ds(0, slabs - 1)]
     copy(6, all_but_one, all_but_one, up).wait_recv()
+    arrived = low_near.at[core]
+    copy(8, arrived, arrived, down_cut).wait_recv()
+    near_pass = copy(9, arrived, arrived, down_cut)
+    near_pass.start()
     parts = coarse[...]
     none = jnp.zeros((1, 8, 128), jnp.float32)
     parts = (
@@ -369,10 +373,6 @@
     padded[pl.ds(3, slabs)] = coarse_solve(jnp.where(iota(parts.shape, 1) < 2, parts, 0.0))
     lifted = prolong_mid(padded[pl.ds(slab, 7)])
     copy(7, near.at[pl.ds(0, 6)], near.at[pl.ds(0, 6)], up).wait_recv()
-    arrived = low_near.at[core]
-    copy(8, arrived, arrived, down_cut).wait_recv()
-    near_pass = copy(9, arrived, arrived, down_cut)
-    near_pass.start()
     near_f = jnp.stack([near[0], near[2], near[4], near[6], near[5], near[3], near[1]])
     near_f = inside(near_f, slab - 3, slabs)
     none = jnp.zeros((1, 32, 128), jnp.float32)
@@ -474,7 +474,7 @@
                 pltpu.SemaphoreType.DMA((14,)),
             ],
             compiler_params=pltpu.CompilerParams(collective_id=0, has_side_effects=True, vmem_limit_bytes=55_900_000),
-        )(orbitals, occupation, state_counts, ion_charge)
+        )(orbitals, pltpu.with_memory_space_constraint(occupation, pltpu.HBM), state_counts, pltpu.with_memory_space_constraint(ion_charge, pltpu.HBM))
 
     return jax.shard_map(
         shards,

time: 46.3 us -> 44.9 us (0.970)
  local copies, waits for them, and re-layouts: 2.05 us -> 1.21 us
  Pallas kernels: 42.8 us -> 42.2 us
    unnamed x6 -> x2, local copies, waits for them, and re-layouts: 2.05 us -> 1.21 us
    pallas_call x1, Pallas kernels: 42.8 us -> 42.2 us  [shards(): pl.pallas_call(functools.partial(kernel, blocks, slabs), out_shape=(jax.S...]
where the time goes in v5:
time: 44.9 us; the launch traced here: 44.7 us
  Pallas kernels  42.2 us (94%)
  between operations  1.28 us (3%)
  local copies, waits for them, and re-layouts  1.21 us (3%)
    pallas_call x1, Pallas kernels, shards(): pl.pallas_call(functools.partial(kernel, blocks, slabs), out_shape=(jax.S...  42.2 us
    unnamed x2, local copies, waits for them, and re-layouts  1.21 us

profile of v5, /device:TPU:1, one launch (start us, length us, event | category | flops | bytes accessed | tf_op | source)
XLA Modules:
  0.0 44.7 jit_solution(9840083474577637165)
XLA Ops:
  1.3 42.2 %shard_map.59 = (f32[4,4096]{1,0:T(4,128)S(1)}, f32[4,128]{1,0:T(4,128)S(1)}) custom-call(bf16[32,4,4096]{2,1,0:T(4,128)(2,1)} %orb_ref.1, s32[1,32]{1,0:T(1,128)} %occ_ref.1, s32[1]{0:T(128)S(6)} %copy.8.count_ref, f32[4,4096]{1,0:T(4,128)} %ion_ref.1), custom_call_target="tpu_custom_call" | custom-call | tf_op jit(solution)/shard_map/pallas_call | solution.py:445
  43.5 0.6 %copy.9 = f32[4,4096]{1,0:T(4,128)} copy(f32[4,4096]{1,0:T(4,128)S(1)} %get-tuple-element.4) | data formatting | bytes 131072
  44.1 0.6 %copy.10 = f32[4,128]{1,0:T(4,128)} copy(f32[4,128]{1,0:T(4,128)S(1)} %get-tuple-element.5) | data formatting | bytes 4096

commit v6 on v5

--- a/solution.py
+++ b/solution.py
@@ -167,7 +167,7 @@
 def kernel(
     blocks, slabs,
     orb_ref, occ_ref, count_ref, ion_ref,
-    pot_ref, kin_ref,
+    out_ref,
     occ, ion, raw, wide, stage, planar, dens, dens_in, field, rims, kin, kin_in,
     near, low_near, own_near, spill, spill_in, coarse, coarse_again, padded, fine,
     load_sem, send_sem, recv_sem,
@@ -416,10 +416,10 @@
     error = inside(relax(guess, mid_cross) + GAIN1 * source[1:5], mid - 1, 2 * slabs)
     fine[...] = direct + relax(prolong_fine(error)[1:7], fine_cross)
     for c in range(blocks):
-        pot_ref[:, c * 128 : (c + 1) * 128] = fine[:, c, :]
+        out_ref[:, c * 128 : (c + 1) * 128] = fine[:, c, :]
 
     copy(10, kin_in.at[pl.ds(0, blocks - 1)], kin_in.at[pl.ds(0, blocks - 1)], down_cut).wait_recv()
-    kin_ref[...] = jnp.sum(kin_in[...], axis=0)
+    out_ref[:, 4096:] = jnp.sum(kin_in[...], axis=0)
 
     copy(0, dens_in.at[pl.ds(0, blocks - 1)], dens_in.at[pl.ds(0, blocks - 1)], down_cut).wait_send()
     for k in range(2):
@@ -442,11 +442,11 @@
     def shards(orbitals, occupation, state_counts, ion_charge):
         f32, bf16 = jnp.float32, jnp.bfloat16
         anywhere, vmem = pl.BlockSpec(memory_space=pl.ANY), pl.BlockSpec(memory_space=pltpu.VMEM)
-        return pl.pallas_call(
+        both = pl.pallas_call(
             functools.partial(kernel, blocks, slabs),
-            out_shape=(jax.ShapeDtypeStruct((4, 4096), f32), jax.ShapeDtypeStruct((4, 128), f32)),
+            out_shape=jax.ShapeDtypeStruct((4, 4224), f32),
             in_specs=[anywhere, anywhere, pl.BlockSpec(memory_space=pltpu.SMEM), anywhere],
-            out_specs=(vmem, vmem),
+            out_specs=vmem,
             scratch_shapes=[
                 pltpu.VMEM((1, 32), jnp.int32),
                 pltpu.VMEM((4, 4096), f32),
@@ -475,6 +475,7 @@
             ],
             compiler_params=pltpu.CompilerParams(collective_id=0, has_side_effects=True, vmem_limit_bytes=55_900_000),
         )(orbitals, pltpu.with_memory_space_constraint(occupation, pltpu.HBM), state_counts, pltpu.with_memory_space_constraint(ion_charge, pltpu.HBM))
+        return both[:, :4096], both[:, 4096:]
 
     return jax.shard_map(
         shards,

time: 44.9 us -> 44.9 us (level)
    slice x0 -> x2, local copies, waits for them, and re-layouts: none -> 1.21 us  [shards(): return (both[:, :4096], both[:, 4096:])]
    unnamed x2 -> x0, local copies, waits for them, and re-layouts: 1.21 us -> none
where the time goes in v6:
time: 44.9 us; the launch traced here: 44.7 us
  Pallas kernels  42.2 us (94%)
  between operations  1.28 us (3%)
  local copies, waits for them, and re-layouts  1.21 us (3%)
    pallas_call x1, Pallas kernels, shards(): pl.pallas_call(functools.partial(kernel, blocks, slabs), out_shape=jax.Sh...  42.2 us
    slice x2, local copies, waits for them, and re-layouts, shards(): return (both[:, :4096], both[:, 4096:])  1.21 us

profile of v6, /device:TPU:1, one launch (start us, length us, event | category | flops | bytes accessed | tf_op | source)
XLA Modules:
  0.0 44.7 jit_solution(599328536540733464)
XLA Ops:
  1.3 42.2 %shard_map.59 = f32[4,4224]{1,0:T(4,128)S(1)} custom-call(bf16[32,4,4096]{2,1,0:T(4,128)(2,1)} %orb_ref.1, s32[1,32]{1,0:T(1,128)} %occ_ref.1, s32[1]{0:T(128)S(6)} %copy.6.count_ref, f32[4,4096]{1,0:T(4,128)} %ion_ref.1), custom_call_target="tpu_custom_call" | custom-call | tf_op jit(solution)/shard_map/pallas_call | solution.py:445
  43.5 0.6 %slice.7 = f32[4,128]{1,0:T(4,128)} slice(f32[4,4224]{1,0:T(4,128)S(1)} %shard_map.59), slice={[0:4], [4096:4224]} | slice | bytes 4096 | tf_op jit(solution)/shard_map/slice | solution.py:478
  44.1 0.6 %slice.6 = f32[4,4096]{1,0:T(4,128)} slice(f32[4,4224]{1,0:T(4,128)S(1)} %shard_map.59), slice={[0:4], [0:4096]} | slice | bytes 131072 | tf_op jit(solution)/shard_map/slice | solution.py:478
